TPU v7x, 32 devices: a whole 2x2x4 slice. The times are simulated.
32 devices in a mesh: groups: 2 (over y), ctx: 4 (over z), tp: 2 (over x), kv: 2 (over core).
Axes of the slice: x: 2, y: 2, z: 4, core: 2. Of those that a mesh axis runs over, the one named last changes fastest.
Arguments:
- queries: bfloat16 [2048, 8192], P(('groups', 'ctx'), ('tp', 'kv')), parts along dimension 0, may hold values from -8 to 8
- key_matrix: bfloat16 [2048, 1024], P(('groups', 'ctx'), 'tp'), parts along dimension 0, may hold values from -8 to 8
- value_matrix: bfloat16 [2048, 1024], P(('groups', 'ctx'), 'tp'), parts along dimension 0, may hold values from -6 to 6
- out_grad: bfloat16 [2048, 8192], P(('groups', 'ctx'), ('tp', 'kv')), parts along dimension 0, may hold values from -6 to 6
- segments: int32 [2048], P(('groups', 'ctx')), parts along dimension 0, may hold values from 0 to 15, never falling along the last dimension, each value on 1 to 512 neighbouring positions
Outputs:
- query_grad: bfloat16 [2048, 8192], P(('groups', 'ctx'), ('tp', 'kv')), parts along dimension 0
- key_gradient: bfloat16 [2048, 1024], P(('groups', 'ctx'), 'tp'), parts along dimension 0
- value_gradient: bfloat16 [2048, 1024], P(('groups', 'ctx'), 'tp'), parts along dimension 0
There are 2 independent parts, one for each index of `groups`. A program takes and returns all parts, laid end to end along the dimension named above; each array names one. Nothing has to cross between parts.
Inputs may be any that keep to these rules, and one draw needn't show every extreme that they name: `segments`: document numbers never fall along the sequence; each of the 16 documents has 1 or more positions and one document holds exactly half of the 1024 positions.
All inputs are finite; a program needn't handle non-finite values.
Results may differ from a plain program's by a relative error of at most 0.011.
Values may be sent and summed in bfloat16 or wider, within the bound.
A program may use at most 64 MiB of HBM per device.

v0:
```python
import jax
import jax.numpy as jnp
from jax import lax
from jax.sharding import PartitionSpec as P

QUERY_HEADS = 64
KEY_VALUE_HEADS = 8
HEAD_SIZE = 128
BLOCK = 128


FILL_LOW = -1e30


def from_behind(array, axis, by):
    count = lax.axis_size(axis)
    return lax.ppermute(array, axis, [(i, (i + by) % count) for i in range(count)])


def swapped(block, axis, apart):
    count = lax.axis_size(axis)
    route = []
    for low in range(count):
        high = low | 1 << apart
        if high != low and high < count:
            route += [(low, high), (high, low)]
    return lax.ppermute(block, axis, route)


def block_scores(row_block, key_block, groups):
    row_count = row_block.shape[0]
    key_count = key_block.shape[0]
    row_view = row_block.reshape(row_count, groups, -1, HEAD_SIZE)
    key_view = key_block.reshape(key_count, groups, HEAD_SIZE)
    scores = jnp.einsum("qgpd,kgd->gpqk", row_view, key_view, preferred_element_type=jnp.float32)
    return scores.reshape(-1, row_count, key_count)


def key_mask(seg_all, q_pos, q_seg, k_first, key_count):
    k_pos = k_first + jnp.arange(key_count, dtype=jnp.int32)
    k_seg = lax.dynamic_slice_in_dim(seg_all, k_first, key_count)
    allowed = (q_seg[:, None] == k_seg[None, :]) & (k_pos[None, :] <= q_pos[:, None])
    active = k_first <= jnp.max(q_pos)
    return (allowed, active)


def stats_update(state_now, query_rows, grad_rows, key_value, allowed, groups, logit_scale):
    peak_old, total_old, weighted_old = state_now
    logits = block_scores(query_rows, key_value[0], groups) * logit_scale
    dprobs = block_scores(grad_rows, key_value[1], groups)
    masked = jnp.where(allowed[None], logits, FILL_LOW)
    peak_new = jnp.maximum(peak_old, jnp.max(masked, axis=-1))
    weights = jnp.where(allowed[None], jnp.exp(masked - peak_new[:, :, None]), 0.0)
    fade = jnp.exp(peak_old - peak_new)
    return (
        peak_new,
        total_old * fade + jnp.sum(weights, axis=-1),
        weighted_old * fade + jnp.sum(weights * dprobs, axis=-1),
    )


def grads_update(query_rows, grad_rows, key_value, allowed, log_total, deltas, groups, logit_scale):
    row_count = query_rows.shape[0]
    key_count = key_value.shape[1]
    logits = block_scores(query_rows, key_value[0], groups) * logit_scale
    dprobs = block_scores(grad_rows, key_value[1], groups)
    shifted = jnp.where(allowed[None], logits - log_total[:, :, None], FILL_LOW)
    probs = jnp.where(allowed[None], jnp.exp(shifted), 0.0)
    dlogits = probs * (dprobs - deltas[:, :, None])
    probs_low = probs.astype(jnp.bfloat16).reshape(groups, -1, row_count, key_count)
    dlogits_low = dlogits.astype(jnp.bfloat16).reshape(groups, -1, row_count, key_count)
    query_view = query_rows.reshape(row_count, groups, -1, HEAD_SIZE)
    grad_view = grad_rows.reshape(row_count, groups, -1, HEAD_SIZE)
    key_view = key_value[0].reshape(key_count, groups, HEAD_SIZE)
    query_term = jnp.einsum(
        "gpqk,kgd->gpqd", dlogits_low, key_view, preferred_element_type=jnp.float32
    )
    key_term = jnp.einsum(
        "gpqk,qgpd->kgd", dlogits_low, query_view, preferred_element_type=jnp.float32
    )
    value_term = jnp.einsum(
        "gpqk,qgpd->kgd", probs_low, grad_view, preferred_element_type=jnp.float32
    )
    return (
        query_term.reshape(-1, row_count, HEAD_SIZE),
        jnp.stack([key_term.reshape(key_count, -1), value_term.reshape(key_count, -1)]),
    )


def visit_stats(
    stats_now, query_rows, grad_rows, q_pos, q_seg, key_value, k_first, seg_all, groups, logit_scale
):
    allowed, active = key_mask(seg_all, q_pos, q_seg, k_first, key_value.shape[1])

    def advance(state_in):
        return stats_update(
            state_in, query_rows, grad_rows, key_value, allowed, groups, logit_scale
        )

    def remain(state_in):
        return state_in

    return lax.cond(active, advance, remain, stats_now)


def visit_grads(
    acc_now,
    kv_grad,
    query_rows,
    grad_rows,
    q_pos,
    q_seg,
    log_total,
    deltas,
    key_value,
    k_first,
    seg_all,
    groups,
    logit_scale,
):
    allowed, active = key_mask(seg_all, q_pos, q_seg, k_first, key_value.shape[1])

    def advance(state_in):
        query_term, kv_term = grads_update(
            query_rows, grad_rows, key_value, allowed, log_total, deltas, groups, logit_scale
        )
        return (state_in[0] + query_term, state_in[1] + kv_term)

    def remain(state_in):
        return state_in

    return lax.cond(active, advance, remain, (acc_now, kv_grad))


def pass_forward(kv_grad):
    return from_behind(kv_grad, "ctx", 1)


def mirror_inputs(stacked, level_list):
    for bit_number in range(level_list):
        stacked = swapped(stacked, "ctx", bit_number)
    return stacked


def mirror_result(block_grad, level_list):
    for bit_number in range(level_list):
        block_grad = swapped(block_grad, "ctx", bit_number)
    return block_grad


def finish_stats(stats_end):
    return (stats_end[0] + jnp.log(stats_end[1]), stats_end[2] / stats_end[1])


def shards(queries, key_matrix, value_matrix, out_grad, segments):
    cycle_size = lax.axis_size("ctx")
    rank_self = lax.axis_index("ctx")
    level_list = cycle_size.bit_length() - 1
    block_count = queries.shape[0] // BLOCK
    head_count = queries.shape[1] // HEAD_SIZE
    group_width = QUERY_HEADS // KEY_VALUE_HEADS
    kv_count = max(head_count // group_width, 1)
    kv_first = lax.axis_index("kv") * head_count // group_width
    logit_scale = HEAD_SIZE ** (-0.5)
    rows_here = block_count * BLOCK
    kept_rows = rows_here - BLOCK
    seg_all = lax.all_gather(segments, "ctx", axis=0, tiled=True)
    arrived = mirror_inputs(jnp.stack([queries[kept_rows:], out_grad[kept_rows:]]), level_list)
    query_rows = jnp.concatenate([queries[:kept_rows], arrived[0]], axis=0)
    grad_rows = jnp.concatenate([out_grad[:kept_rows], arrived[1]], axis=0)
    offsets = jnp.arange(BLOCK, dtype=jnp.int32)
    moved_first = ((cycle_size - 1 - rank_self) * block_count + block_count - 1) * BLOCK
    q_pos = jnp.concatenate(
        [rank_self * rows_here + jnp.arange(kept_rows, dtype=jnp.int32), moved_first + offsets]
    )
    q_seg = jnp.concatenate(
        [
            lax.dynamic_slice_in_dim(seg_all, rank_self * rows_here, kept_rows),
            lax.dynamic_slice_in_dim(seg_all, moved_first, BLOCK),
        ]
    )
    key_value = jnp.stack(
        [
            lax.dynamic_slice_in_dim(key_matrix, kv_first * HEAD_SIZE, kv_count * HEAD_SIZE, 1),
            lax.dynamic_slice_in_dim(value_matrix, kv_first * HEAD_SIZE, kv_count * HEAD_SIZE, 1),
        ]
    )
    start_stats = (
        jnp.full((head_count, rows_here), FILL_LOW, jnp.float32),
        jnp.zeros((head_count, rows_here), jnp.float32),
        jnp.zeros((head_count, rows_here), jnp.float32),
    )
    start_acc = jnp.zeros((head_count, rows_here, HEAD_SIZE), jnp.float32)

    def see_stats(stats_now, part_kv, k_first):
        return visit_stats(
            stats_now,
            query_rows,
            grad_rows,
            q_pos,
            q_seg,
            part_kv,
            k_first,
            seg_all,
            kv_count,
            logit_scale,
        )

    def see_grads(acc_now, kv_grad, part_kv, k_first, log_total, deltas):
        return visit_grads(
            acc_now,
            kv_grad,
            query_rows,
            grad_rows,
            q_pos,
            q_seg,
            log_total,
            deltas,
            part_kv,
            k_first,
            seg_all,
            kv_count,
            logit_scale,
        )

    stats_now = see_stats(start_stats, key_value, rank_self * rows_here)

    def fwd_turn(turn_index, state_now):
        moving, stats_in = state_now
        moving = from_behind(moving, "ctx", 1)
        anchor = (rank_self - turn_index) % cycle_size
        return (moving, see_stats(stats_in, moving, anchor * rows_here))

    log_total, deltas = finish_stats(
        lax.fori_loop(1, cycle_size, fwd_turn, (key_value, stats_now))[1]
    )
    empty_grad = jnp.zeros((2, rows_here, kv_count * HEAD_SIZE), jnp.float32)
    grad_acc, kv_grad = see_grads(
        start_acc, empty_grad, key_value, rank_self * rows_here, log_total, deltas
    )

    def back_turn(turn_index, state_now):
        moving, kv_now, acc_now = state_now
        moving = from_behind(moving, "ctx", 1)
        kv_now = pass_forward(kv_now)
        anchor = (rank_self - turn_index) % cycle_size
        acc_now, kv_now = see_grads(acc_now, kv_now, moving, anchor * rows_here, log_total, deltas)
        return (moving, kv_now, acc_now)

    loop_end = lax.fori_loop(1, cycle_size, back_turn, (key_value, kv_grad, grad_acc))
    grad_acc = loop_end[2]
    key_value_grad = pass_forward(loop_end[1])
    grad_full = jnp.zeros((2, rows_here, key_matrix.shape[1]), jnp.float32)
    grad_full = lax.dynamic_update_slice_in_dim(grad_full, key_value_grad, kv_first * HEAD_SIZE, 2)
    summed = lax.psum(grad_full.astype(jnp.bfloat16), "kv").astype(jnp.float32)
    key_gradient = (summed[0] * logit_scale).astype(jnp.bfloat16)
    value_gradient = summed[1].astype(jnp.bfloat16)
    query_all = (
        (grad_acc * logit_scale)
        .astype(jnp.bfloat16)
        .transpose(1, 0, 2)
        .reshape(rows_here, head_count * HEAD_SIZE)
    )
    returned = mirror_result(query_all[kept_rows:], level_list)
    return (
        jnp.concatenate([query_all[:kept_rows], returned], axis=0),
        key_gradient,
        value_gradient,
    )


def solution(mesh):
    return jax.shard_map(
        shards,
        mesh=mesh,
        in_specs=(
            P(("groups", "ctx"), ("tp", "kv")),
            P(("groups", "ctx"), "tp"),
            P(("groups", "ctx"), "tp"),
            P(("groups", "ctx"), ("tp", "kv")),
            P(("groups", "ctx")),
        ),
        out_specs=(
            P(("groups", "ctx"), ("tp", "kv")),
            P(("groups", "ctx"), "tp"),
            P(("groups", "ctx"), "tp"),
        ),
        check_vma=False,
    )
```

profile of v0, /device:TPU:0, one launch (start us, length us, event | category | flops | bytes accessed | tf_op | source)
XLA Modules:
  0.0 302.5 jit_solution(5921494750152145410)
XLA Ops:
  11.4 3.1 %collective-permute-start.3 = (bf16[2,128,2048]{1,2,0:T(8,128)(2,1)}, bf16[2,128,2048]{1,2,0:T(8,128)(2,1)}, u32[]{:S(2)}, u32[]{:S(2)}) collective-permute-start(bf16[2,128,2048]{1,2,0:T(8,128)(2,1)} %pad_maximum_fusion.1), channel_id=1, source_target_pairs={{0,4},{4,0},{8,12},{12,8},{1,5},{5,1},{9,13},{13,9},{2,6},{6,2},{1... | collective-permute-start | bytes 3145736 | tf_op jit(solution)/shard_map/ppermute | solution.py:27
  14.5 23.5 %collective-permute-done.3 = bf16[2,128,2048]{1,2,0:T(8,128)(2,1)} collective-permute-done((bf16[2,128,2048]{1,2,0:T(8,128)(2,1)}, bf16[2,128,2048]{1,2,0:T(8,128)(2,1)}, u32[]{:S(2)}, u32[]{:S(2)}) %collective-permute-start.3) | collective-permute-done | bytes 1048608 | tf_op jit(solution)/shard_map/ppermute | solution.py:27
  37.9 2.8 collective-permute-start.4
  44.9 23.5 %all-gather = s32[4,1,256]{2,1,0:T(1,128)S(1)} all-gather(s32[1,1,256]{2,1,0:T(1,128)S(1)} %bitcast.244), channel_id=1, replica_groups=mesh['groups'=2,'ctx'=4,'tp'=2,'kv'=2] {'ctx'}, dimensions={0}, use_global_device_ids=true | all-gather | bytes 5120 | tf_op jit(solution)/shard_map/all_gather | solution.py:167
  69.6 16.4 %collective-permute-done.4 = bf16[2,128,2048]{1,2,0:T(8,128)(2,1)} collective-permute-done((bf16[2,128,2048]{1,2,0:T(8,128)(2,1)}, bf16[2,128,2048]{1,2,0:T(8,128)(2,1)}, u32[]{:S(2)}, u32[]{:S(2)}) %collective-permute-start.4) | collective-permute-done | bytes 1048608 | tf_op jit(solution)/shard_map/ppermute | solution.py:27
  89.1 1.5 copy.108
  90.6 11.5 %conditional.4 = (f32[16,256]{1,0:T(8,128)}, f32[16,256]{1,0:T(8,128)S(1)}, f32[16,256]{1,0:T(8,128)}) conditional(s32[]{:T(128)} %convert_element_type.59, () %tuple.93, (pred[256,256]{0,1:T(8,128)(4,1)S(1)}, bf16[256,256]{1,0:T(8,128)(2,1)S(1)}, bf16[256,2048]{0,1:T(8,128)(2,1)S(1)}, bf16[256,256]{1,0:T(8,128)(2,1)S(1)}, ...), branch_computations={%region_2.3_spmd, %region_3.7_spmd} | conditional | flops 551571456 | bytes 32669748 | solution.py:103
  91.3 3.7 %fusion.1 = (f32[2,8,256]{2,1,0:T(8,128)S(1)}, f32[2,256,256,8]{2,1,3,0:T(8,128)}) fusion(pred[256,256]{0,1:T(8,128)(4,1)S(1)} %get-tuple-element.740, bf16[256,2,8,128]{0,3,2,1:T(8,128)(2,1)S(1)} %bitcast.196, bf16[256,2,128,1]{2,1,0,3:T(2,128)(2,1)} %bitcast.226), kind=kOutput, calls=%fused_computation.4 | convolution fusion | flops 271577088 | bytes 5455872 | tf_op jit(solution)/shard_map/cond/branch_1_fun/qgpd,kgd->gpqk/dot_general | solution.py:35
  95.7 4.1 %fusion = f32[2,8,256]{2,1,0:T(8,128)S(1)} fusion(f32[2,256,256,8]{2,1,3,0:T(8,128)} %get-tuple-element.942, bf16[256,2,8,128]{0,3,2,1:T(8,128)(2,1)} %bitcast.213, f32[2,8,256]{2,1,0:T(8,128)S(1)} %broadcast_maximum_fusion, pred[256,256]{0,1:T(8,128)(4,1)S(1)} %get-tuple-element.740, bf16[256,2,128,1]{2,1,0,3:T(2,128)(2,1)} %bitcast.231), kind=kOutput, calls=%fused_computation.1 | convolution fusion | flops 274722816 | bytes 5472256 | tf_op jit(solution)/shard_map/cond/branch_1_fun/qgpd,kgd->gpqk/dot_general | solution.py:35
  102.1 60.2 %while.40 = (s32[]{:T(128)}, bf16[2,256,256]{1,2,0:T(8,128)(2,1)}, f32[16,256]{1,0:T(8,128)}, f32[16,256]{1,0:T(8,128)S(1)}, f32[16,256]{1,0:T(8,128)}, /*index=...) while((s32[]{:T(128)}, bf16[2,256,256]{1,2,0:T(8,128)(2,1)}, ...), condition=%wide.region_13.14_spmd, body=%wide.region_7.13_spmd.sunk | while | flops 551760128 | bytes 21800464 | solution.py:235
  102.2 3.1 %collective-permute-start = (bf16[2,256,256]{1,2,0:T(8,128)(2,1)}, bf16[2,256,256]{1,2,0:T(8,128)(2,1)S(1)}, u32[]{:S(2)}, u32[]{:S(2)}) collective-permute-start(bf16[2,256,256]{1,2,0:T(8,128)(2,1)} %get-tuple-element.1159), channel_id=1, source_target_pairs={{0,4},{4,8},{8,12},{12,0},{1,5},{5,9},{9,13},{13,1},{2,6},{6,10},{... | collective-permute-start | bytes 786440 | tf_op jit(solution)/shard_map/while/body/eval_jaxpr/ppermute | solution.py:17
  105.2 9.1 %collective-permute-done = bf16[2,256,256]{1,2,0:T(8,128)(2,1)S(1)} collective-permute-done((bf16[2,256,256]{1,2,0:T(8,128)(2,1)}, bf16[2,256,256]{1,2,0:T(8,128)(2,1)S(1)}, u32[]{:S(2)}, u32[]{:S(2)}) %collective-permute-start) | collective-permute-done | bytes 262176 | tf_op jit(solution)/shard_map/while/body/eval_jaxpr/ppermute | solution.py:17
  114.9 9.1 %conditional.8 = ((f32[16,256]{1,0:T(8,128)}, f32[16,256]{1,0:T(8,128)S(1)}, f32[16,256]{1,0:T(8,128)})) conditional(s32[]{:T(128)} %convert_element_type.79, (f32[16,256]{1,0:T(8,128)}, f32[16,256]{1,0:T(8,128)S(1)}, f32[16,256]{1,0:T(8,128)}) %tuple.140, (s32[256]{0:T(256)}, s32[]{:T(128)}, s32[1024]{0:T(1024)}, s32[1,256]{1,0:T(1,128)}, ...), branch_computations={%region_8.8_spmd, %region_9.12_spmd} | conditional | flops 551760128 | bytes 20226122 | solution.py:103
  120.5 1.6 fusion.7
  122.1 1.4 bitcast_add_fusion.2
  124.7 8.5 %collective-permute-done = bf16[2,256,256]{1,2,0:T(8,128)(2,1)S(1)} collective-permute-done((bf16[2,256,256]{1,2,0:T(8,128)(2,1)}, bf16[2,256,256]{1,2,0:T(8,128)(2,1)S(1)}, u32[]{:S(2)}, u32[]{:S(2)}) %collective-permute-start) | collective-permute-done | bytes 262176 | tf_op jit(solution)/shard_map/while/body/eval_jaxpr/ppermute | solution.py:17
  133.8 9.1 %conditional.8 = ((f32[16,256]{1,0:T(8,128)}, f32[16,256]{1,0:T(8,128)S(1)}, f32[16,256]{1,0:T(8,128)})) conditional(s32[]{:T(128)} %convert_element_type.79, (f32[16,256]{1,0:T(8,128)}, f32[16,256]{1,0:T(8,128)S(1)}, f32[16,256]{1,0:T(8,128)}) %tuple.140, (s32[256]{0:T(256)}, s32[]{:T(128)}, s32[1024]{0:T(1024)}, s32[1,256]{1,0:T(1,128)}, ...), branch_computations={%region_8.8_spmd, %region_9.12_spmd} | conditional | flops 551760128 | bytes 20226122 | solution.py:103
  139.3 1.6 fusion.7
  141.0 1.4 bitcast_add_fusion.2
  143.6 8.4 %collective-permute-done = bf16[2,256,256]{1,2,0:T(8,128)(2,1)S(1)} collective-permute-done((bf16[2,256,256]{1,2,0:T(8,128)(2,1)}, bf16[2,256,256]{1,2,0:T(8,128)(2,1)S(1)}, u32[]{:S(2)}, u32[]{:S(2)}) %collective-permute-start) | collective-permute-done | bytes 262176 | tf_op jit(solution)/shard_map/while/body/eval_jaxpr/ppermute | solution.py:17
  152.6 9.1 %conditional.8 = ((f32[16,256]{1,0:T(8,128)}, f32[16,256]{1,0:T(8,128)S(1)}, f32[16,256]{1,0:T(8,128)})) conditional(s32[]{:T(128)} %convert_element_type.79, (f32[16,256]{1,0:T(8,128)}, f32[16,256]{1,0:T(8,128)S(1)}, f32[16,256]{1,0:T(8,128)}) %tuple.140, (s32[256]{0:T(256)}, s32[]{:T(128)}, s32[1024]{0:T(1024)}, s32[1,256]{1,0:T(1,128)}, ...), branch_computations={%region_8.8_spmd, %region_9.12_spmd} | conditional | flops 551760128 | bytes 20226122 | solution.py:103
  158.1 1.6 fusion.7
  163.2 11.5 %conditional.5 = (f32[16,256,128]{2,1,0:T(8,128)S(1)}, f32[2,256,256]{1,2,0:T(8,128)}) conditional(s32[]{:T(128)} %convert_element_type.59, () %tuple.92, (pred[256,256]{0,1:T(8,128)(4,1)}, bf16[256,256]{1,0:T(8,128)(2,1)}, bf16[256,2048]{0,1:T(8,128)(2,1)S(1)}, f32[16,256]{1,0:T(8,128)S(1)}, bf16[256,256]{1,0:T(8,128)(2,1)S(1)}, ...), branch_computations={%region_14.15_spmd, %region_15.16_spmd} | conditional | flops 1354891264 | bytes 49070180 | solution.py:132
  164.4 2.7 fusion.25
  167.1 3.8 %fusion.14 = bf16[2,8,256,256]{2,3,1,0:T(8,128)(2,1)S(1)} fusion(f32[2,256,256,8]{2,1,3,0:T(8,128)} %fusion.25, bf16[256,2,8,128]{0,3,2,1:T(8,128)(2,1)S(1)} %bitcast.214, f32[2,8,256]{2,1,0:T(8,128)S(1)} %bitcast.238, f32[2,8,256]{2,1,0:T(8,128)S(1)} %bitcast.240, pred[256,256]{0,1:T(8,128)(4,1)S(1)} %copy-done.7, bf16[256,2,128,1]{2,1,0,3:T(2,128)(2,1)S(1)} %bitcast.232), kind=kOutput, calls=%fused_computation.31 | convolution fusion | flops 275775488 | bytes 7569408 | tf_op jit(solution)/shard_map/cond/branch_1_fun/qgpd,kgd->gpqk/dot_general | solution.py:35
  174.7 84.7 %while.41 = (s32[]{:T(128)}, bf16[2,256,256]{1,2,0:T(8,128)(2,1)}, f32[2,256,256]{1,2,0:T(8,128)}, f32[16,256,128]{2,1,0:T(8,128)S(1)}, s32[]{:T(128)}, /*index=...) while((s32[]{:T(128)}, bf16[2,256,256]{1,2,0:T(8,128)(2,1)}, ...), condition=%wide.region_19.20_spmd, body=%wide.region_16.19_spmd.sunk | while | flops 1355743488 | bytes 43640408 | solution.py:250
  174.9 17.6 %collective-permute-done.1 = bf16[2,256,256]{1,2,0:T(8,128)(2,1)S(1)} collective-permute-done((bf16[2,256,256]{1,2,0:T(8,128)(2,1)}, bf16[2,256,256]{1,2,0:T(8,128)(2,1)S(1)}, u32[]{:S(2)}, u32[]{:S(2)}) %collective-permute-start.1) | collective-permute-done | bytes 262176 | tf_op jit(solution)/shard_map/while/body/eval_jaxpr/ppermute | solution.py:17
  193.2 8.6 %conditional.9 = ((f32[16,256,128]{2,1,0:T(8,128)S(1)}, f32[2,256,256]{1,2,0:T(8,128)})) conditional(s32[]{:T(128)} %convert_element_type.80, (f32[16,256,128]{2,1,0:T(8,128)S(1)}, f32[2,256,256]{1,2,0:T(8,128)}) %tuple.143, (s32[256]{0:T(256)S(1)}, s32[]{:T(128)}, s32[1024]{0:T(1024)}, s32[1,256]{1,0:T(1,128)S(1)}, s32[256]{0:T(256)S(1)}, ...), branch_computations={%region_17.17_spmd, %region_18.18_spmd} | conditional | flops 1355743488 | bytes 38920288 | solution.py:132
  195.0 1.6 fusion.31
  198.5 1.9 maximum_add_fusion
  201.8 1.9 copy.235
  203.7 17.0 %collective-permute-done.1 = bf16[2,256,256]{1,2,0:T(8,128)(2,1)S(1)} collective-permute-done((bf16[2,256,256]{1,2,0:T(8,128)(2,1)}, bf16[2,256,256]{1,2,0:T(8,128)(2,1)S(1)}, u32[]{:S(2)}, u32[]{:S(2)}) %collective-permute-start.1) | collective-permute-done | bytes 262176 | tf_op jit(solution)/shard_map/while/body/eval_jaxpr/ppermute | solution.py:17
  221.4 8.6 %conditional.9 = ((f32[16,256,128]{2,1,0:T(8,128)S(1)}, f32[2,256,256]{1,2,0:T(8,128)})) conditional(s32[]{:T(128)} %convert_element_type.80, (f32[16,256,128]{2,1,0:T(8,128)S(1)}, f32[2,256,256]{1,2,0:T(8,128)}) %tuple.143, (s32[256]{0:T(256)S(1)}, s32[]{:T(128)}, s32[1024]{0:T(1024)}, s32[1,256]{1,0:T(1,128)S(1)}, s32[256]{0:T(256)S(1)}, ...), branch_computations={%region_17.17_spmd, %region_18.18_spmd} | conditional | flops 1355743488 | bytes 38920288 | solution.py:132
  223.2 1.6 fusion.31
  226.7 1.9 maximum_add_fusion
  230.0 1.9 copy.235
  231.9 16.2 %collective-permute-done.1 = bf16[2,256,256]{1,2,0:T(8,128)(2,1)S(1)} collective-permute-done((bf16[2,256,256]{1,2,0:T(8,128)(2,1)}, bf16[2,256,256]{1,2,0:T(8,128)(2,1)S(1)}, u32[]{:S(2)}, u32[]{:S(2)}) %collective-permute-start.1) | collective-permute-done | bytes 262176 | tf_op jit(solution)/shard_map/while/body/eval_jaxpr/ppermute | solution.py:17
  248.9 8.6 %conditional.9 = ((f32[16,256,128]{2,1,0:T(8,128)S(1)}, f32[2,256,256]{1,2,0:T(8,128)})) conditional(s32[]{:T(128)} %convert_element_type.80, (f32[16,256,128]{2,1,0:T(8,128)S(1)}, f32[2,256,256]{1,2,0:T(8,128)}) %tuple.143, (s32[256]{0:T(256)S(1)}, s32[]{:T(128)}, s32[1024]{0:T(1024)}, s32[1,256]{1,0:T(1,128)S(1)}, s32[256]{0:T(256)S(1)}, ...), branch_computations={%region_17.17_spmd, %region_18.18_spmd} | conditional | flops 1355743488 | bytes 38920288 | solution.py:132
  250.7 1.6 fusion.31
  254.2 1.9 maximum_add_fusion
  257.5 1.9 copy.235
  261.2 9.4 %collective-permute-done.7 = bf16[2,256,256]{2,1,0:T(8,128)(2,1)S(1)} collective-permute-done((bf16[2,256,256]{2,1,0:T(8,128)(2,1)S(1)}, bf16[2,256,256]{2,1,0:T(8,128)(2,1)S(1)}, u32[]{:S(2)}, u32[]{:S(2)}) %collective-permute-start.7) | collective-permute-done | bytes 262176 | tf_op jit(solution)/shard_map/ppermute | solution.py:17
  271.6 5.0 %collective-permute-done.5 = bf16[128,2048]{1,0:T(8,128)(2,1)S(1)} collective-permute-done((bf16[128,2048]{1,0:T(8,128)(2,1)S(1)}, bf16[128,2048]{1,0:T(8,128)(2,1)S(1)}, u32[]{:S(2)}, u32[]{:S(2)}) %collective-permute-start.5) | collective-permute-done | bytes 524320 | tf_op jit(solution)/shard_map/ppermute | solution.py:27
  276.5 5.0 %collective-permute-start.6 = (bf16[128,2048]{1,0:T(8,128)(2,1)S(1)}, bf16[128,2048]{1,0:T(8,128)(2,1)S(1)}, u32[]{:S(2)}, u32[]{:S(2)}) collective-permute-start(bf16[128,2048]{1,0:T(8,128)(2,1)S(1)} %collective-permute-done.5), channel_id=1, source_target_pairs={{0,8},{8,0},{4,12},{12,4},{1,9},{9,1},{5,13},{13,5},{2,10},{10,2},... | collective-permute-start | bytes 1572872 | tf_op jit(solution)/shard_map/ppermute | solution.py:27
  281.7 6.8 %all-reduce.2.cloned.1.call-done = bf16[2,256,512]{2,1,0:T(8,128)(2,1)} async-done(((bf16[2,256,512]{2,1,0:T(8,128)(2,1)}), bf16[2,256,512]{2,1,0:T(8,128)(2,1)}) %all-reduce.2.cloned.1.call-update) | async-done | bytes 524304 | tf_op jit(solution)/shard_map/psum | solution.py:255
  288.5 1.7 fusion.43
  290.2 1.7 slice_bitcast_fusion.4
  291.9 2.7 collective-permute-done.6
  (167 shorter events, 65.3 us)
Async XLA Ops:
  7.2 281.3 %all-reduce.2.cloned.1.call-start = ((), (), s32[]{:S(2)}) async-start(), calls=%async_computation | async-start | bytes 1048576 | tf_op jit(solution)/shard_map/psum | solution.py:255
  8.5 35.4 %copy-start.13 = (bf16[256,512]{1,0:T(8,128)(2,1)S(1)}, bf16[256,512]{1,0:T(8,128)(2,1)}, u32[]{:S(2)}) copy-start(bf16[256,512]{1,0:T(8,128)(2,1)} %param.19) | copy-start | bytes 786436
  8.5 35.4 %copy-start.14 = (bf16[256,512]{1,0:T(8,128)(2,1)S(1)}, bf16[256,512]{1,0:T(8,128)(2,1)}, u32[]{:S(2)}) copy-start(bf16[256,512]{1,0:T(8,128)(2,1)} %param.18) | copy-start | bytes 786436
  10.1 34.8 %copy-start.16 = (s32[256]{0:T(256)S(1)}, s32[256]{0:T(256)}, u32[]{:S(2)}) copy-start(s32[256]{0:T(256)} %param.21) | copy-start | bytes 3076
  11.4 26.5 %collective-permute-start.3 = (bf16[2,128,2048]{1,2,0:T(8,128)(2,1)}, bf16[2,128,2048]{1,2,0:T(8,128)(2,1)}, u32[]{:S(2)}, u32[]{:S(2)}) collective-permute-start(bf16[2,128,2048]{1,2,0:T(8,128)(2,1)} %pad_maximum_fusion.1), channel_id=1, source_target_pairs={{0,4},{4,0},{8,12},{12,8},{1,5},{5,1},{9,13},{13,9},{2,6},{6,2},{1... | collective-permute-start | bytes 3145736 | tf_op jit(solution)/shard_map/ppermute | solution.py:27
  37.9 48.1 %collective-permute-start.4 = (bf16[2,128,2048]{1,2,0:T(8,128)(2,1)}, bf16[2,128,2048]{1,2,0:T(8,128)(2,1)}, u32[]{:S(2)}, u32[]{:S(2)}) collective-permute-start(bf16[2,128,2048]{1,2,0:T(8,128)(2,1)} %collective-permute-done.3), channel_id=1, source_target_pairs={{0,8},{8,0},{4,12},{12,4},{1,9},{9,1},{5,13},{13,5},{2,10},{10,2},... | collective-permute-start | bytes 3145736 | tf_op jit(solution)/shard_map/ppermute | solution.py:27
  43.9 46.7 %copy-start.4 = (bf16[256,256]{1,0:T(8,128)(2,1)}, bf16[256,256]{1,0:T(8,128)(2,1)S(1)}, u32[]{:S(2)}) copy-start(bf16[256,256]{1,0:T(8,128)(2,1)S(1)} %get-tuple-element.956) | copy-start | bytes 393220
  44.1 25.1 %copy-start.8 = (bf16[2,256,256]{1,2,0:T(8,128)(2,1)}, bf16[2,256,256]{1,2,0:T(8,128)(2,1)S(1)}, u32[]{:S(2)}) copy-start(bf16[2,256,256]{1,2,0:T(8,128)(2,1)S(1)} %pad_maximum_fusion.5) | copy-start | bytes 786436
  68.4 0.6 copy-start.15
  69.0 0.6 copy-start.9
  69.0 0.6 copy-start.11
  69.6 21.0 %copy-start.6 = (pred[256,256]{0,1:T(8,128)(4,1)}, pred[256,256]{0,1:T(8,128)(4,1)S(1)}, u32[]{:S(2)}) copy-start(pred[256,256]{0,1:T(8,128)(4,1)S(1)} %compare_and_fusion.2) | copy-start | bytes 196612
  95.7 4.7 %copy-start = (f32[2,256,256,8]{2,1,3,0:T(8,128)S(1)}, f32[2,256,256,8]{2,1,3,0:T(8,128)}, u32[]{:S(2)}) copy-start(f32[2,256,256,8]{2,1,3,0:T(8,128)} %get-tuple-element.942) | copy-start | bytes 12582916 | tf_op jit(solution)/shard_map/cond
  102.2 12.2 %collective-permute-start = (bf16[2,256,256]{1,2,0:T(8,128)(2,1)}, bf16[2,256,256]{1,2,0:T(8,128)(2,1)S(1)}, u32[]{:S(2)}, u32[]{:S(2)}) collective-permute-start(bf16[2,256,256]{1,2,0:T(8,128)(2,1)} %get-tuple-element.1159), channel_id=1, source_target_pairs={{0,4},{4,8},{8,12},{12,0},{1,5},{5,9},{9,13},{13,1},{2,6},{6,10},{... | collective-permute-start | bytes 786440 | tf_op jit(solution)/shard_map/while/body/eval_jaxpr/ppermute | solution.py:17
  124.7 8.5 %collective-permute-start = (bf16[2,256,256]{1,2,0:T(8,128)(2,1)}, bf16[2,256,256]{1,2,0:T(8,128)(2,1)S(1)}, u32[]{:S(2)}, u32[]{:S(2)}) collective-permute-start(bf16[2,256,256]{1,2,0:T(8,128)(2,1)} %get-tuple-element.1159), channel_id=1, source_target_pairs={{0,4},{4,8},{8,12},{12,0},{1,5},{5,9},{9,13},{13,1},{2,6},{6,10},{... | collective-permute-start | bytes 786440 | tf_op jit(solution)/shard_map/while/body/eval_jaxpr/ppermute | solution.py:17
  143.6 8.4 %collective-permute-start = (bf16[2,256,256]{1,2,0:T(8,128)(2,1)}, bf16[2,256,256]{1,2,0:T(8,128)(2,1)S(1)}, u32[]{:S(2)}, u32[]{:S(2)}) collective-permute-start(bf16[2,256,256]{1,2,0:T(8,128)(2,1)} %get-tuple-element.1159), channel_id=1, source_target_pairs={{0,4},{4,8},{8,12},{12,0},{1,5},{5,9},{9,13},{13,1},{2,6},{6,10},{... | collective-permute-start | bytes 786440 | tf_op jit(solution)/shard_map/while/body/eval_jaxpr/ppermute | solution.py:17
  163.1 11.6 %copy-start.10 = (s32[256]{0:T(256)S(1)}, s32[256]{0:T(256)}, u32[]{:S(2)}) copy-start(s32[256]{0:T(256)} %get-tuple-element.1266) | copy-start | bytes 3076
  163.1 11.6 %copy-start.12 = (s32[256]{0:T(256)S(1)}, s32[256]{0:T(256)}, u32[]{:S(2)}) copy-start(s32[256]{0:T(256)} %get-tuple-element.1267) | copy-start | bytes 3076
  163.4 3.7 %copy-start.2 = (bf16[256,2048]{0,1:T(8,128)(2,1)S(1)}, bf16[256,2048]{0,1:T(8,128)(2,1)}, u32[]{:S(2)}) copy-start(bf16[256,2048]{0,1:T(8,128)(2,1)} %get-tuple-element.777) | copy-start | bytes 3145732 | tf_op jit(solution)/shard_map/cond
  163.4 3.7 %copy-start.7 = (pred[256,256]{0,1:T(8,128)(4,1)S(1)}, pred[256,256]{0,1:T(8,128)(4,1)}, u32[]{:S(2)}) copy-start(pred[256,256]{0,1:T(8,128)(4,1)} %get-tuple-element.772) | copy-start | bytes 196612 | tf_op jit(solution)/shard_map/cond
  167.1 4.6 %copy-start.1 = (f32[2,256,256,8]{2,1,3,0:T(8,128)S(1)}, f32[2,256,256,8]{2,1,3,0:T(8,128)}, u32[]{:S(2)}) copy-start(f32[2,256,256,8]{2,1,3,0:T(8,128)} %fusion.25) | copy-start | bytes 12582916 | tf_op jit(solution)/shard_map/cond
  174.7 18.5 %collective-permute-start.2 = (f32[2,256,256]{1,2,0:T(8,128)}, f32[2,256,256]{1,2,0:T(8,128)}, u32[]{:S(2)}, u32[]{:S(2)}) collective-permute-start(f32[2,256,256]{1,2,0:T(8,128)} %get-tuple-element.1216), channel_id=1, source_target_pairs={{0,4},{4,8},{8,12},{12,0},{1,5},{5,9},{9,13},{13,1},{2,6},{6,10},{... | collective-permute-start | bytes 1572872 | tf_op jit(solution)/shard_map/while/body/eval_jaxpr/ppermute | solution.py:17
  174.8 17.7 %collective-permute-start.1 = (bf16[2,256,256]{1,2,0:T(8,128)(2,1)}, bf16[2,256,256]{1,2,0:T(8,128)(2,1)S(1)}, u32[]{:S(2)}, u32[]{:S(2)}) collective-permute-start(bf16[2,256,256]{1,2,0:T(8,128)(2,1)} %get-tuple-element.1215), channel_id=1, source_target_pairs={{0,4},{4,8},{8,12},{12,0},{1,5},{5,9},{9,13},{13,1},{2,6},{6,10},{... | collective-permute-start | bytes 786440 | tf_op jit(solution)/shard_map/while/body/eval_jaxpr/ppermute | solution.py:17
  193.2 1.8 copy-start.3
  203.7 17.7 %collective-permute-start.2 = (f32[2,256,256]{1,2,0:T(8,128)}, f32[2,256,256]{1,2,0:T(8,128)}, u32[]{:S(2)}, u32[]{:S(2)}) collective-permute-start(f32[2,256,256]{1,2,0:T(8,128)} %get-tuple-element.1216), channel_id=1, source_target_pairs={{0,4},{4,8},{8,12},{12,0},{1,5},{5,9},{9,13},{13,1},{2,6},{6,10},{... | collective-permute-start | bytes 1572872 | tf_op jit(solution)/shard_map/while/body/eval_jaxpr/ppermute | solution.py:17
  203.7 17.0 %collective-permute-start.1 = (bf16[2,256,256]{1,2,0:T(8,128)(2,1)}, bf16[2,256,256]{1,2,0:T(8,128)(2,1)S(1)}, u32[]{:S(2)}, u32[]{:S(2)}) collective-permute-start(bf16[2,256,256]{1,2,0:T(8,128)(2,1)} %get-tuple-element.1215), channel_id=1, source_target_pairs={{0,4},{4,8},{8,12},{12,0},{1,5},{5,9},{9,13},{13,1},{2,6},{6,10},{... | collective-permute-start | bytes 786440 | tf_op jit(solution)/shard_map/while/body/eval_jaxpr/ppermute | solution.py:17
  221.4 1.8 copy-start.3
  231.9 16.9 %collective-permute-start.2 = (f32[2,256,256]{1,2,0:T(8,128)}, f32[2,256,256]{1,2,0:T(8,128)}, u32[]{:S(2)}, u32[]{:S(2)}) collective-permute-start(f32[2,256,256]{1,2,0:T(8,128)} %get-tuple-element.1216), channel_id=1, source_target_pairs={{0,4},{4,8},{8,12},{12,0},{1,5},{5,9},{9,13},{13,1},{2,6},{6,10},{... | collective-permute-start | bytes 1572872 | tf_op jit(solution)/shard_map/while/body/eval_jaxpr/ppermute | solution.py:17
  231.9 16.2 %collective-permute-start.1 = (bf16[2,256,256]{1,2,0:T(8,128)(2,1)}, bf16[2,256,256]{1,2,0:T(8,128)(2,1)S(1)}, u32[]{:S(2)}, u32[]{:S(2)}) collective-permute-start(bf16[2,256,256]{1,2,0:T(8,128)(2,1)} %get-tuple-element.1215), channel_id=1, source_target_pairs={{0,4},{4,8},{8,12},{12,0},{1,5},{5,9},{9,13},{13,1},{2,6},{6,10},{... | collective-permute-start | bytes 786440 | tf_op jit(solution)/shard_map/while/body/eval_jaxpr/ppermute | solution.py:17
  248.9 1.8 copy-start.3
  260.9 9.8 %collective-permute-start.7 = (bf16[2,256,256]{2,1,0:T(8,128)(2,1)S(1)}, bf16[2,256,256]{2,1,0:T(8,128)(2,1)S(1)}, u32[]{:S(2)}, u32[]{:S(2)}) collective-permute-start(bf16[2,256,256]{2,1,0:T(8,128)(2,1)S(1)} %copy.111), channel_id=1, source_target_pairs={{0,4},{4,8},{8,12},{12,0},{1,5},{5,9},{9,13},{13,1},{2,6},{6,10},{... | collective-permute-start | bytes 786440 | tf_op jit(solution)/shard_map/ppermute | solution.py:17
  261.2 15.4 %collective-permute-start.5 = (bf16[128,2048]{1,0:T(8,128)(2,1)S(1)}, bf16[128,2048]{1,0:T(8,128)(2,1)S(1)}, u32[]{:S(2)}, u32[]{:S(2)}) collective-permute-start(bf16[128,2048]{1,0:T(8,128)(2,1)S(1)} %bitcast.227), channel_id=1, source_target_pairs={{0,4},{4,0},{8,12},{12,8},{1,5},{5,1},{9,13},{13,9},{2,6},{6,2},{1... | collective-permute-start | bytes 1572872 | tf_op jit(solution)/shard_map/ppermute | solution.py:27
  270.7 0.8 copy-start.5
  276.5 18.0 %collective-permute-start.6 = (bf16[128,2048]{1,0:T(8,128)(2,1)S(1)}, bf16[128,2048]{1,0:T(8,128)(2,1)S(1)}, u32[]{:S(2)}, u32[]{:S(2)}) collective-permute-start(bf16[128,2048]{1,0:T(8,128)(2,1)S(1)} %collective-permute-done.5), channel_id=1, source_target_pairs={{0,8},{8,0},{4,12},{12,4},{1,9},{9,1},{5,13},{13,5},{2,10},{10,2},... | collective-permute-start | bytes 1572872 | tf_op jit(solution)/shard_map/ppermute | solution.py:27
Sparse Core Ops, SparseCore 0:
  271.7 16.7 all-reduce.1
where the time goes:
time: 304 us; the launch traced here: 302 us
  waiting for transfers between devices  141 us (46%)
  matrix products  40.4 us (13%)
  local copies, waits for them, and re-layouts  35.2 us (12%)
  other arithmetic  32.1 us (11%)
  blocking collectives  23.5 us (8%)
  between operations  15.7 us (5%)
  starting transfers between devices  14.2 us (5%)
    ppermute x10, waiting for transfers between devices, from_behind(): lax.ppermute(array, axis, [(i, (i + by) % count) for i in range(count)])  86.2 us
    ppermute x4, waiting for transfers between devices, swapped(): return lax.ppermute(block, axis, route)  47.6 us
    dot_general x16, matrix products, block_scores(): jnp.einsum('qgpd,kgd->gpqk', row_view, key_view, preferred_element_type=j...  29 us
    all_gather x1, blocking collectives, shards(): seg_all = lax.all_gather(segments, 'ctx', axis=0, tiled=True)  23.5 us
    ppermute x4, starting transfers between devices, swapped(): return lax.ppermute(block, axis, route)  10.9 us
    while x9, local copies, waits for them, and re-layouts  9.88 us
    add x6, other arithmetic, advance(): return (state_in[0] + query_term, state_in[1] + kv_term)  7.14 us
    psum x1, waiting for transfers between devices, shards(): summed = lax.psum(grad_full.astype(jnp.bfloat16), 'kv').astype(jnp.float32)  6.79 us
  transfers between devices with their start and end apart: 15, of which 12 were waited for; matrix products, arithmetic and copies ran while one was open for 3% of the time, Pallas kernels for 0%

commit v1 on v0

v1 whole, which is shorter than its diff:
```python
import functools
import jax
import jax.numpy as jnp
from jax import lax
from jax.experimental import pallas as pl
from jax.experimental.pallas import tpu as pltpu
from jax.sharding import PartitionSpec as P

QUERY_HEADS = 64
KEY_VALUE_HEADS = 8
HEAD_SIZE = 128
HALF = 128
LOG2E = 1.4426950408889634
NEG = -1e30
MESH = pl.DeviceIdType.MESH
NT = (((1,), (1,)), ((), ()))


def kernel(
    n, reach, rows, per_kv, kv_count, shared,
    q_hbm, k_hbm, v_hbm, g_hbm, seg_ref,
    dq_hbm, dk_hbm, dv_hbm,
    qv, gv, dqv, win, segwin, segcol, bias, kt, acc, sendb, ret, fin, pfin,
    load_sem, own_sem, seg_send, seg_recv, send_sem, recv_sem, back_send, back_recv,
    pair_send, pair_recv, dq_sem, out_sem,
):
    rank = lax.axis_index("ctx")
    kv = lax.axis_index("kv")
    up = lax.rem(rank + 1, n)
    down = lax.rem(rank + n - 1, n)
    mate = 1 - kv
    scale = HEAD_SIZE ** -0.5
    width = reach * rows + HALF
    halves = rows // HALF
    first = 0 if shared else kv * kv_count
    mate_first = 0 if shared else mate * kv_count

    def cols(base, g):
        if shared:
            return pl.ds(g * HEAD_SIZE, HEAD_SIZE)
        return pl.ds(pl.multiple_of((base + g) * HEAD_SIZE, HEAD_SIZE), HEAD_SIZE)

    def slot(d):
        return pl.ds((reach - d) * rows, rows)

    loads = [
        pltpu.make_async_copy(q_hbm, qv, load_sem.at[0]),
        pltpu.make_async_copy(g_hbm, gv, load_sem.at[1]),
    ]
    owns = []
    for g in range(kv_count):
        for t, ref in ((0, k_hbm), (1, v_hbm)):
            owns.append(
                pltpu.make_async_copy(
                    ref.at[:, cols(first, g)], win.at[t, g, slot(0)], own_sem.at[t, g]
                )
            )

    def forward(t, g, d):
        ref = k_hbm if t == 0 else v_hbm
        src = ref.at[:, cols(first, g)] if d == 0 else win.at[t, g, slot(d)]
        return pltpu.make_async_remote_copy(
            src_ref=src,
            dst_ref=win.at[t, g, slot(d + 1)],
            send_sem=send_sem.at[t, g, d],
            recv_sem=recv_sem.at[t, g, d + 1],
            device_id={"ctx": up},
            device_id_type=MESH,
        )

    def forward_seg(d):
        return pltpu.make_async_remote_copy(
            src_ref=seg_ref if d == 0 else segwin.at[d],
            dst_ref=segwin.at[d + 1],
            send_sem=seg_send.at[d],
            recv_sem=seg_recv.at[d + 1],
            device_id={"ctx": up},
            device_id_type=MESH,
        )

    def back(g, d):
        return pltpu.make_async_remote_copy(
            src_ref=sendb.at[g, d - 1],
            dst_ref=ret.at[g, d - 1],
            send_sem=back_send.at[g, d - 1],
            recv_sem=back_recv.at[g, d - 1],
            device_id={"ctx": down},
            device_id_type=MESH,
        )

    def to_mate(g):
        return pltpu.make_async_remote_copy(
            src_ref=fin.at[g],
            dst_ref=pfin.at[g],
            send_sem=pair_send.at[g],
            recv_sem=pair_recv.at[g],
            device_id={"kv": mate},
            device_id_type=MESH,
        )

    has_up = rank < n - 1

    for copy in loads + owns:
        copy.start()

    barrier = pltpu.get_barrier_semaphore()
    pl.semaphore_signal(barrier, inc=1, device_id={"kv": mate}, device_id_type=MESH)

    @pl.when(has_up)
    def _():
        pl.semaphore_signal(barrier, inc=1, device_id={"ctx": up}, device_id_type=MESH)

    @pl.when(rank > 0)
    def _():
        pl.semaphore_signal(barrier, inc=1, device_id={"ctx": down}, device_id_type=MESH)

    expected = 1 + jnp.where(has_up, 1, 0) + jnp.where(rank > 0, 1, 0)
    pl.semaphore_wait(barrier, expected)

    @pl.when(has_up)
    def _():
        forward_seg(0).start()
        forward(0, 0, 0).start()
        forward(1, 0, 0).start()

    for d in range(1, reach + 1):
        @pl.when(rank < d)
        def _(d=d):
            for g in range(kv_count):
                for t in range(2):
                    win[t, g, slot(d), :] = jnp.zeros((rows, HEAD_SIZE), jnp.bfloat16)
            segwin[d] = jnp.full((1, rows), -1, jnp.int32)

    acc[...] = jnp.zeros_like(acc)

    def pass_on_seg():
        for d in range(1, reach + 1):
            @pl.when(rank >= d)
            def _(d=d):
                forward_seg(d - 1).wait_recv()

            if d < reach:
                @pl.when((rank >= d) & has_up)
                def _(d=d):
                    forward_seg(d).start()

    def pass_on(g):
        for d in range(1, reach):
            for t in range(2):
                @pl.when(rank >= d)
                def _(d=d, t=t):
                    forward(t, g, d - 1).wait_recv()

                @pl.when((rank >= d) & has_up)
                def _(d=d, t=t):
                    forward(t, g, d).start()

    def last_slot(g):
        @pl.when(rank >= reach)
        def _():
            for t in range(2):
                forward(t, g, reach - 1).wait_recv()

    def send_own(g):
        @pl.when(has_up)
        def _():
            for t in range(2):
                forward(t, g, 0).start()

    def make_bias():
        for d in range(reach + 1):
            row = (seg_ref[...] if d == 0 else segwin[d]).astype(jnp.float32)
            segcol[slot(d), :] = jnp.broadcast_to(row, (HALF, rows)).T
        key_at = lax.broadcasted_iota(jnp.int32, (width, HALF), 0)
        query_at = lax.broadcasted_iota(jnp.int32, (width, HALF), 1)
        causal = key_at <= query_at + reach * rows
        for h in range(halves):
            seg_q = seg_ref[:, h * HALF:(h + 1) * HALF].astype(jnp.float32)
            same = segcol[h * HALF:h * HALF + width, :] == seg_q
            bias[h] = jnp.where(same & causal, 0.0, NEG)

    def unit(g, h, p):
        span = slice(h * HALF, h * HALF + width)
        part = slice(h * HALF, (h + 1) * HALF)
        c0 = pl.multiple_of((g * per_kv + 2 * p) * HEAD_SIZE, HEAD_SIZE)
        c1 = pl.multiple_of((g * per_kv + 2 * p + 1) * HEAD_SIZE, HEAD_SIZE)
        one, two = pl.ds(c0, HEAD_SIZE), pl.ds(c1, HEAD_SIZE)
        qu = jnp.concatenate([qv[part, one], qv[part, two]], axis=0)
        gu = jnp.concatenate([gv[part, one], gv[part, two]], axis=0)
        s = lax.dot_general(win[0, g, span, :], qu, NT, preferred_element_type=jnp.float32)
        dp = lax.dot_general(win[1, g, span, :], gu, NT, preferred_element_type=jnp.float32)
        b = bias[h]
        s = s + jnp.concatenate([b, b], axis=1)
        peak = jnp.max(s, axis=0, keepdims=True)
        e = jnp.exp2((s - peak) * (scale * LOG2E))
        inv = 1.0 / jnp.sum(e, axis=0, keepdims=True)
        delta = jnp.sum(e * dp, axis=0, keepdims=True) * inv
        pn = e * inv
        ds = (pn * (dp - delta)).astype(jnp.bfloat16)
        pb = pn.astype(jnp.bfloat16)
        dqt = jnp.dot(kt[g, :, span], ds, preferred_element_type=jnp.float32)
        dq = (dqt * scale).T.astype(jnp.bfloat16)
        dqv[part, one] = dq[:HALF]
        dqv[part, two] = dq[HALF:]
        acc[g, 0, span, :] += jnp.dot(ds, qu, preferred_element_type=jnp.float32)
        acc[g, 1, span, :] += jnp.dot(pb, gu, preferred_element_type=jnp.float32)

    def units(g, begin, end):
        def body(p, carry):
            for h in range(halves):
                unit(g, h, p)
            return carry

        lax.fori_loop(begin, end, body, 0)

    def send_back(g, d):
        if d < reach:
            @pl.when(has_up & (rank >= d))
            def _():
                back(g, d + 1).wait_recv()
                sendb[g, d - 1] = (
                    acc[g, :, slot(d), :] + ret[g, d].astype(jnp.float32)
                ).astype(jnp.bfloat16)

            @pl.when(jnp.logical_not(has_up) & (rank >= d))
            def _():
                sendb[g, d - 1] = acc[g, :, slot(d), :].astype(jnp.bfloat16)
        else:
            @pl.when(rank >= d)
            def _():
                sendb[g, d - 1] = acc[g, :, slot(d), :].astype(jnp.bfloat16)

        @pl.when(rank >= d)
        def _():
            back(g, d).start()

    def finish(g):
        @pl.when(has_up)
        def _():
            back(g, 1).wait_recv()
            for t in range(2):
                acc[g, t, slot(0), :] += ret[g, 0, t].astype(jnp.float32)

        for t in range(2):
            factor = scale if t == 0 else 1.0
            fin[g, t] = (acc[g, t, slot(0), :] * factor).astype(jnp.bfloat16)
        to_mate(g).start()

    pass_on_seg()
    make_bias()
    pass_on(0)
    for copy in loads + owns:
        copy.wait()
    split = per_kv // 4
    for g in range(kv_count):
        if g + 1 < kv_count:
            send_own(g + 1)
        last_slot(g)
        kt[g] = win[0, g].T
        units(g, 0, split)
        if g + 1 < kv_count:
            pass_on(g + 1)
        if g > 0:
            for d in range(reach - 1, 0, -1):
                send_back(g - 1, d)
        units(g, split, per_kv // 2)
        send_back(g, reach)
        wide = pl.ds(g * per_kv * HEAD_SIZE, per_kv * HEAD_SIZE)
        pltpu.make_async_copy(dqv.at[:, wide], dq_hbm.at[:, wide], dq_sem.at[g]).start()
    for d in range(reach - 1, 0, -1):
        send_back(kv_count - 1, d)
    for g in range(kv_count):
        finish(g)

    outs = []
    for g in range(kv_count):
        to_mate(g).wait()
        if shared:
            for t in range(2):
                pfin[g, t] = (
                    fin[g, t].astype(jnp.float32) + pfin[g, t].astype(jnp.float32)
                ).astype(jnp.bfloat16)
        for t, ref in ((0, dk_hbm), (1, dv_hbm)):
            outs.append(
                pltpu.make_async_copy(
                    pfin.at[g, t], ref.at[:, cols(mate_first, g)], out_sem.at[0, t, g]
                )
            )
            if not shared:
                outs.append(
                    pltpu.make_async_copy(
                        fin.at[g, t], ref.at[:, cols(first, g)], out_sem.at[1, t, g]
                    )
                )
                outs[-1].start()
                outs[-2].start()
            else:
                outs[-1].start()
    for g in range(kv_count):
        wide = pl.ds(g * per_kv * HEAD_SIZE, per_kv * HEAD_SIZE)
        pltpu.make_async_copy(dqv.at[:, wide], dq_hbm.at[:, wide], dq_sem.at[g]).wait()
    for copy in outs:
        copy.wait()
    for d in range(reach):
        @pl.when(has_up & (rank >= d))
        def _(d=d):
            forward_seg(d).wait_send()
            for g in range(kv_count):
                for t in range(2):
                    forward(t, g, d).wait_send()
    for d in range(1, reach + 1):
        @pl.when(rank >= d)
        def _(d=d):
            for g in range(kv_count):
                back(g, d).wait_send()


def shards(queries, key_matrix, value_matrix, out_grad, segments):
    n = lax.axis_size("ctx")
    rows = queries.shape[0]
    head_count = queries.shape[1] // HEAD_SIZE
    group_width = QUERY_HEADS // KEY_VALUE_HEADS
    kv_count = max(head_count // group_width, 1)
    per_kv = head_count // kv_count
    kv_here = key_matrix.shape[1] // HEAD_SIZE
    shared = kv_here < kv_count * lax.axis_size("kv")
    reach = n // 2
    window = (reach + 1) * rows
    width = reach * rows + HALF
    bf16, f32 = jnp.bfloat16, jnp.float32
    dma = pltpu.SemaphoreType.DMA
    anywhere = pl.BlockSpec(memory_space=pl.ANY)
    return pl.pallas_call(
        functools.partial(kernel, n, reach, rows, per_kv, kv_count, shared),
        out_shape=(
            jax.ShapeDtypeStruct(queries.shape, bf16),
            jax.ShapeDtypeStruct(key_matrix.shape, bf16),
            jax.ShapeDtypeStruct(value_matrix.shape, bf16),
        ),
        in_specs=[anywhere] * 4 + [pl.BlockSpec(memory_space=pltpu.VMEM)],
        out_specs=(anywhere,) * 3,
        scratch_shapes=[
            pltpu.VMEM(queries.shape, bf16),
            pltpu.VMEM(queries.shape, bf16),
            pltpu.VMEM(queries.shape, bf16),
            pltpu.VMEM((2, kv_count, window, HEAD_SIZE), bf16),
            pltpu.VMEM((reach + 1, 1, rows), jnp.int32),
            pltpu.VMEM((window, HALF), f32),
            pltpu.VMEM((rows // HALF, width, HALF), f32),
            pltpu.VMEM((kv_count, HEAD_SIZE, window), bf16),
            pltpu.VMEM((kv_count, 2, window, HEAD_SIZE), f32),
            pltpu.VMEM((kv_count, reach, 2, rows, HEAD_SIZE), bf16),
            pltpu.VMEM((kv_count, reach, 2, rows, HEAD_SIZE), bf16),
            pltpu.VMEM((kv_count, 2, rows, HEAD_SIZE), bf16),
            pltpu.VMEM((kv_count, 2, rows, HEAD_SIZE), bf16),
            dma((2,)),
            dma((2, kv_count)),
            dma((reach + 1,)),
            dma((reach + 1,)),
            dma((2, kv_count, reach + 1)),
            dma((2, kv_count, reach + 1)),
            dma((kv_count, reach)),
            dma((kv_count, reach)),
            dma((kv_count,)),
            dma((kv_count,)),
            dma((kv_count,)),
            dma((2, 2, kv_count)),
        ],
        compiler_params=pltpu.CompilerParams(
            collective_id=0, has_side_effects=True, vmem_limit_bytes=60 * 1024 * 1024
        ),
    )(queries, key_matrix, value_matrix, out_grad, segments.reshape(1, rows))


def solution(mesh):
    return jax.shard_map(
        shards,
        mesh=mesh,
        in_specs=(
            P(("groups", "ctx"), ("tp", "kv")),
            P(("groups", "ctx"), "tp"),
            P(("groups", "ctx"), "tp"),
            P(("groups", "ctx"), ("tp", "kv")),
            P(("groups", "ctx")),
        ),
        out_specs=(
            P(("groups", "ctx"), ("tp", "kv")),
            P(("groups", "ctx"), "tp"),
            P(("groups", "ctx"), "tp"),
        ),
        check_vma=False,
    )
```

time: 304 us -> 46.8 us (0.15)
  waiting for transfers between devices: 141 us -> 0 us
  Pallas kernels: 0 us -> 41.9 us
  matrix products: 40.4 us -> 0 us
  other arithmetic: 32.1 us -> 0 us
  local copies, waits for them, and re-layouts: 35.2 us -> 4.1 us
  blocking collectives: 23.5 us -> 0 us
  between operations: 15.7 us -> 0.65 us
  starting transfers between devices: 14.2 us -> 0 us
    ppermute x14 -> x0, waiting for transfers between devices: 134 us -> none  [the longest x10 86.2 us: from_behind(): lax.ppermute(array, axis, [(i, (i + by) % count) for i in range(count)])]
    pallas_call x0 -> x1, Pallas kernels: none -> 41.9 us  [shards(): pl.pallas_call(functools.partial(kernel, n, reach, rows, per_kv, kv_count...]
    dot_general x28 -> x0, matrix products: 40.4 us -> none  [the longest x16 29 us: block_scores(): jnp.einsum('qgpd,kgd->gpqk', row_view, key_view, preferred_element_type=j...]
    all_gather x1 -> x0, blocking collectives: 23.5 us -> none  [shards(): seg_all = lax.all_gather(segments, 'ctx', axis=0, tiled=True)]
    add x20 -> x0, other arithmetic: 15.9 us -> none  [the longest x6 7.14 us: advance(): return (state_in[0] + query_term, state_in[1] + kv_term)]
    ppermute x14 -> x0, starting transfers between devices: 14.1 us -> none  [the longest x4 10.9 us: swapped(): return lax.ppermute(block, axis, route)]
    while x12 -> x0, local copies, waits for them, and re-layouts: 13.2 us -> none
    psum x1 -> x0, waiting for transfers between devices: 6.79 us -> none  [shards(): summed = lax.psum(grad_full.astype(jnp.bfloat16), 'kv').astype(jnp.float32)]
  transfers between devices with their start and end apart: 15 -> 0, of which waited for: 12 -> 0; matrix products, arithmetic and copies ran while one was open for 3% -> 0% of each run, Pallas kernels for 0% -> 0%
where the time goes in v1:
time: 46.8 us; the launch traced here: 46.6 us
  Pallas kernels  41.9 us (90%)
  local copies, waits for them, and re-layouts  4.1 us (9%)
  between operations  0.65 us (1%)
    pallas_call x1, Pallas kernels, shards(): pl.pallas_call(functools.partial(kernel, n, reach, rows, per_kv, kv_count...  41.9 us
    unnamed x7, local copies, waits for them, and re-layouts  4.1 us

profile of v1, /device:TPU:0, one launch (start us, length us, event | category | flops | bytes accessed | tf_op | source)
XLA Modules:
  0.0 46.6 jit_solution(16294999594754359728)
XLA Ops:
  0.6 41.9 %shard_map.76 = (bf16[256,2048]{1,0:T(8,128)(2,1)}, bf16[256,512]{1,0:T(8,128)(2,1)}, bf16[256,512]{1,0:T(8,128)(2,1)}) custom-call(bf16[256,2048]{1,0:T(8,128)(2,1)} %q_hbm.1, bf16[256,512]{1,0:T(8,128)(2,1)} %k_hbm.1, bf16[256,512]{1,0:T(8,128)(2,1)} %v_hbm.1, bf16[256,2048]{1,0:T(8,128)(2,1)} %g_hbm.1, s32[1,256]{1,0:T(1,128)} %bitcast.1), custom_call_target="tpu_custom_call" | custom-call | tf_op jit(solution)/shard_map/pallas_call | solution.py:333
  42.5 0.0 copy-start.1
  42.5 2.3 %copy.11 = bf16[256,2048]{1,0:T(8,128)(2,1)} copy(bf16[256,2048]{1,0:T(8,128)(2,1)} %get-tuple-element.6) | data formatting | bytes 2097152
  44.9 0.0 copy-done.1
  44.9 0.0 copy-start
  44.9 0.7 %copy.12 = bf16[256,512]{1,0:T(8,128)(2,1)} copy(bf16[256,512]{1,0:T(8,128)(2,1)S(1)} %copy-done.1) | data formatting | bytes 524288
  45.6 0.3 copy-done
  45.9 0.7 %copy.13 = bf16[256,512]{1,0:T(8,128)(2,1)} copy(bf16[256,512]{1,0:T(8,128)(2,1)S(1)} %copy-done) | data formatting | bytes 524288
Async XLA Ops:
  42.5 2.4 %copy-start.1 = (bf16[256,512]{1,0:T(8,128)(2,1)S(1)}, bf16[256,512]{1,0:T(8,128)(2,1)}, u32[]{:S(2)}) copy-start(bf16[256,512]{1,0:T(8,128)(2,1)} %get-tuple-element.7) | copy-start | bytes 786436
  44.9 1.0 %copy-start = (bf16[256,512]{1,0:T(8,128)(2,1)S(1)}, bf16[256,512]{1,0:T(8,128)(2,1)}, u32[]{:S(2)}) copy-start(bf16[256,512]{1,0:T(8,128)(2,1)} %get-tuple-element.8) | copy-start | bytes 786436

commit v2 on v1

--- a/solution.py
+++ b/solution.py
@@ -10,6 +10,7 @@
 KEY_VALUE_HEADS = 8
 HEAD_SIZE = 128
 HALF = 128
+CHUNK = 32
 LOG2E = 1.4426950408889634
 NEG = -1e30
 MESH = pl.DeviceIdType.MESH
@@ -18,11 +19,11 @@
 
 def kernel(
     n, reach, rows, per_kv, kv_count, shared,
-    q_hbm, k_hbm, v_hbm, g_hbm, seg_ref,
-    dq_hbm, dk_hbm, dv_hbm,
-    qv, gv, dqv, win, segwin, segcol, bias, kt, acc, sendb, ret, fin, pfin,
+    q_hbm, k_hbm, v_hbm, g_hbm, seg_hbm,
+    dqv, fin, other,
+    qv, gv, sv, dpv, peaks, pv, dsv, win, segwin, segcol, bias, kt, acc, sendb, ret, pfin,
     load_sem, own_sem, seg_send, seg_recv, send_sem, recv_sem, back_send, back_recv,
-    pair_send, pair_recv, dq_sem, out_sem,
+    pair_send, pair_recv,
 ):
     rank = lax.axis_index("ctx")
     kv = lax.axis_index("kv")
@@ -33,7 +34,6 @@
     width = reach * rows + HALF
     halves = rows // HALF
     first = 0 if shared else kv * kv_count
-    mate_first = 0 if shared else mate * kv_count
 
     def cols(base, g):
         if shared:
@@ -47,6 +47,7 @@
         pltpu.make_async_copy(q_hbm, qv, load_sem.at[0]),
         pltpu.make_async_copy(g_hbm, gv, load_sem.at[1]),
     ]
+    seg_load = pltpu.make_async_copy(seg_hbm, segwin.at[0], load_sem.at[2])
     owns = []
     for g in range(kv_count):
         for t, ref in ((0, k_hbm), (1, v_hbm)):
@@ -70,7 +71,7 @@
 
     def forward_seg(d):
         return pltpu.make_async_remote_copy(
-            src_ref=seg_ref if d == 0 else segwin.at[d],
+            src_ref=seg_hbm if d == 0 else segwin.at[d],
             dst_ref=segwin.at[d + 1],
             send_sem=seg_send.at[d],
             recv_sem=seg_recv.at[d + 1],
@@ -100,7 +101,7 @@
 
     has_up = rank < n - 1
 
-    for copy in loads + owns:
+    for copy in [seg_load] + owns + loads:
         copy.start()
 
     barrier = pltpu.get_barrier_semaphore()
@@ -169,49 +170,101 @@
 
     def make_bias():
         for d in range(reach + 1):
-            row = (seg_ref[...] if d == 0 else segwin[d]).astype(jnp.float32)
+            row = segwin[d].astype(jnp.float32)
             segcol[slot(d), :] = jnp.broadcast_to(row, (HALF, rows)).T
         key_at = lax.broadcasted_iota(jnp.int32, (width, HALF), 0)
         query_at = lax.broadcasted_iota(jnp.int32, (width, HALF), 1)
         causal = key_at <= query_at + reach * rows
         for h in range(halves):
-            seg_q = seg_ref[:, h * HALF:(h + 1) * HALF].astype(jnp.float32)
+            seg_q = segwin[0, :, h * HALF:(h + 1) * HALF].astype(jnp.float32)
             same = segcol[h * HALF:h * HALF + width, :] == seg_q
             bias[h] = jnp.where(same & causal, 0.0, NEG)
 
-    def unit(g, h, p):
-        span = slice(h * HALF, h * HALF + width)
-        part = slice(h * HALF, (h + 1) * HALF)
+    def spot(g, h, p):
         c0 = pl.multiple_of((g * per_kv + 2 * p) * HEAD_SIZE, HEAD_SIZE)
         c1 = pl.multiple_of((g * per_kv + 2 * p + 1) * HEAD_SIZE, HEAD_SIZE)
-        one, two = pl.ds(c0, HEAD_SIZE), pl.ds(c1, HEAD_SIZE)
-        qu = jnp.concatenate([qv[part, one], qv[part, two]], axis=0)
-        gu = jnp.concatenate([gv[part, one], gv[part, two]], axis=0)
-        s = lax.dot_general(win[0, g, span, :], qu, NT, preferred_element_type=jnp.float32)
-        dp = lax.dot_general(win[1, g, span, :], gu, NT, preferred_element_type=jnp.float32)
+        part = slice(h * HALF, (h + 1) * HALF)
+        return part, pl.ds(c0, HEAD_SIZE), pl.ds(c1, HEAD_SIZE)
+
+    def pair(ref, g, h, p):
+        part, one, two = spot(g, h, p)
+        return jnp.concatenate([ref[part, one], ref[part, two]], axis=0)
+
+    def span(h):
+        return slice(h * HALF, h * HALF + width)
+
+    def products(g, h, p):
+        s = lax.dot_general(
+            win[0, g, span(h), :], pair(qv, g, h, p), NT, preferred_element_type=jnp.float32
+        )
         b = bias[h]
         s = s + jnp.concatenate([b, b], axis=1)
-        peak = jnp.max(s, axis=0, keepdims=True)
-        e = jnp.exp2((s - peak) * (scale * LOG2E))
-        inv = 1.0 / jnp.sum(e, axis=0, keepdims=True)
-        delta = jnp.sum(e * dp, axis=0, keepdims=True) * inv
-        pn = e * inv
-        ds = (pn * (dp - delta)).astype(jnp.bfloat16)
-        pb = pn.astype(jnp.bfloat16)
-        dqt = jnp.dot(kt[g, :, span], ds, preferred_element_type=jnp.float32)
+        sv[h] = s
+        peaks[h] = jnp.max(s, axis=0, keepdims=True)
+        dpv[h] = lax.dot_general(
+            win[1, g, span(h), :], pair(gv, g, h, p), NT, preferred_element_type=jnp.float32
+        )
+
+    def softmax(h):
+        peak = peaks[h]
+        total = jnp.zeros((8, 2 * HALF), jnp.float32)
+        weighted = jnp.zeros((8, 2 * HALF), jnp.float32)
+        for c in range(0, width, CHUNK):
+            rows_c = slice(c, c + CHUNK)
+            e = jnp.exp2((sv[h, rows_c, :] - peak) * (scale * LOG2E))
+            sv[h, rows_c, :] = e
+            total = total + jnp.sum(e.reshape(-1, 8, 2 * HALF), axis=0)
+            weighted = weighted + jnp.sum(
+                (e * dpv[h, rows_c, :]).reshape(-1, 8, 2 * HALF), axis=0
+            )
+        inv = 1.0 / jnp.sum(total, axis=0, keepdims=True)
+        delta = jnp.sum(weighted, axis=0, keepdims=True) * inv
+        for c in range(0, width, CHUNK):
+            rows_c = slice(c, c + CHUNK)
+            pn = sv[h, rows_c, :] * inv
+            dsv[h, rows_c, :] = (pn * (dpv[h, rows_c, :] - delta)).astype(jnp.bfloat16)
+            pv[h, rows_c, :] = pn.astype(jnp.bfloat16)
+
+    def grads(g, h, p):
+        part, one, two = spot(g, h, p)
+        ds = dsv[h]
+        dqt = jnp.dot(kt[g, :, span(h)], ds, preferred_element_type=jnp.float32)
         dq = (dqt * scale).T.astype(jnp.bfloat16)
         dqv[part, one] = dq[:HALF]
         dqv[part, two] = dq[HALF:]
-        acc[g, 0, span, :] += jnp.dot(ds, qu, preferred_element_type=jnp.float32)
-        acc[g, 1, span, :] += jnp.dot(pb, gu, preferred_element_type=jnp.float32)
+        acc[g, 0, span(h), :] += jnp.dot(
+            ds, pair(qv, g, h, p), preferred_element_type=jnp.float32
+        )
+        acc[g, 1, span(h), :] += jnp.dot(
+            pv[h], pair(gv, g, h, p), preferred_element_type=jnp.float32
+        )
+
+    pairs = per_kv // 2
+    last_half = halves - 1
+
+    def begin_units(g):
+        dsv[last_half] = jnp.zeros((width, 2 * HALF), jnp.bfloat16)
+        pv[last_half] = jnp.zeros((width, 2 * HALF), jnp.bfloat16)
+        products(g, 0, 0)
 
     def units(g, begin, end):
         def body(p, carry):
             for h in range(halves):
-                unit(g, h, p)
+                if h < last_half:
+                    products(g, h + 1, p)
+                else:
+                    products(g, 0, jnp.minimum(p + 1, pairs - 1))
+                softmax(h)
+                if h > 0:
+                    grads(g, h - 1, p)
+                else:
+                    grads(g, last_half, jnp.maximum(p - 1, 0))
             return carry
 
         lax.fori_loop(begin, end, body, 0)
+
+    def end_units(g):
+        grads(g, last_half, pairs - 1)
 
     def send_back(g, d):
         if d < reach:
@@ -247,6 +300,7 @@
         to_mate(g).start()
 
     pass_on_seg()
+    seg_load.wait()
     make_bias()
     pass_on(0)
     for copy in loads + owns:
@@ -257,50 +311,30 @@
             send_own(g + 1)
         last_slot(g)
         kt[g] = win[0, g].T
+        begin_units(g)
         units(g, 0, split)
         if g + 1 < kv_count:
             pass_on(g + 1)
         if g > 0:
             for d in range(reach - 1, 0, -1):
                 send_back(g - 1, d)
-        units(g, split, per_kv // 2)
+        units(g, split, pairs)
+        end_units(g)
         send_back(g, reach)
-        wide = pl.ds(g * per_kv * HEAD_SIZE, per_kv * HEAD_SIZE)
-        pltpu.make_async_copy(dqv.at[:, wide], dq_hbm.at[:, wide], dq_sem.at[g]).start()
     for d in range(reach - 1, 0, -1):
         send_back(kv_count - 1, d)
     for g in range(kv_count):
         finish(g)
 
-    outs = []
     for g in range(kv_count):
         to_mate(g).wait()
-        if shared:
-            for t in range(2):
-                pfin[g, t] = (
+        for t in range(2):
+            if shared:
+                other[g, t] = (
                     fin[g, t].astype(jnp.float32) + pfin[g, t].astype(jnp.float32)
                 ).astype(jnp.bfloat16)
-        for t, ref in ((0, dk_hbm), (1, dv_hbm)):
-            outs.append(
-                pltpu.make_async_copy(
-                    pfin.at[g, t], ref.at[:, cols(mate_first, g)], out_sem.at[0, t, g]
-                )
-            )
-            if not shared:
-                outs.append(
-                    pltpu.make_async_copy(
-                        fin.at[g, t], ref.at[:, cols(first, g)], out_sem.at[1, t, g]
-                    )
-                )
-                outs[-1].start()
-                outs[-2].start()
             else:
-                outs[-1].start()
-    for g in range(kv_count):
-        wide = pl.ds(g * per_kv * HEAD_SIZE, per_kv * HEAD_SIZE)
-        pltpu.make_async_copy(dqv.at[:, wide], dq_hbm.at[:, wide], dq_sem.at[g]).wait()
-    for copy in outs:
-        copy.wait()
+                other[g, t] = pfin[g, t]
     for d in range(reach):
         @pl.when(has_up & (rank >= d))
         def _(d=d):
@@ -315,6 +349,27 @@
                 back(g, d).wait_send()
 
 
+def place(kv_count, shared, dqv, fin, other, dq_hbm, dk_hbm, dv_hbm, sem):
+    kv = lax.axis_index("kv")
+    copies = [pltpu.make_async_copy(dqv, dq_hbm, sem.at[0])]
+    parts = [(other, 0)] if shared else [(fin, kv * kv_count), (other, (1 - kv) * kv_count)]
+    for source, base in parts:
+        for g in range(kv_count):
+            start = g * HEAD_SIZE
+            if not shared:
+                start = pl.multiple_of((base + g) * HEAD_SIZE, HEAD_SIZE)
+            for t, ref in ((0, dk_hbm), (1, dv_hbm)):
+                copies.append(
+                    pltpu.make_async_copy(
+                        source.at[g, t], ref.at[:, pl.ds(start, HEAD_SIZE)], sem.at[len(copies)]
+                    )
+                )
+    for copy in copies:
+        copy.start()
+    for copy in copies:
+        copy.wait()
+
+
 def shards(queries, key_matrix, value_matrix, out_grad, segments):
     n = lax.axis_size("ctx")
     rows = queries.shape[0]
@@ -327,33 +382,38 @@
     reach = n // 2
     window = (reach + 1) * rows
     width = reach * rows + HALF
+    halves = rows // HALF
     bf16, f32 = jnp.bfloat16, jnp.float32
     dma = pltpu.SemaphoreType.DMA
-    anywhere = pl.BlockSpec(memory_space=pl.ANY)
-    return pl.pallas_call(
+    anywhere = pl.BlockSpec(memory_space=pltpu.HBM)
+    inner = pltpu.VMEM
+    dqv, fin, other = pl.pallas_call(
         functools.partial(kernel, n, reach, rows, per_kv, kv_count, shared),
         out_shape=(
-            jax.ShapeDtypeStruct(queries.shape, bf16),
-            jax.ShapeDtypeStruct(key_matrix.shape, bf16),
-            jax.ShapeDtypeStruct(value_matrix.shape, bf16),
+            inner(queries.shape, bf16),
+            inner((kv_count, 2, rows, HEAD_SIZE), bf16),
+            inner((kv_count, 2, rows, HEAD_SIZE), bf16),
         ),
-        in_specs=[anywhere] * 4 + [pl.BlockSpec(memory_space=pltpu.VMEM)],
-        out_specs=(anywhere,) * 3,
+        in_specs=[anywhere] * 5,
+        out_specs=(pl.BlockSpec(memory_space=pltpu.VMEM),) * 3,
         scratch_shapes=[
             pltpu.VMEM(queries.shape, bf16),
             pltpu.VMEM(queries.shape, bf16),
-            pltpu.VMEM(queries.shape, bf16),
+            pltpu.VMEM((halves, width, 2 * HALF), f32),
+            pltpu.VMEM((halves, width, 2 * HALF), f32),
+            pltpu.VMEM((halves, 1, 2 * HALF), f32),
+            pltpu.VMEM((halves, width, 2 * HALF), bf16),
+            pltpu.VMEM((halves, width, 2 * HALF), bf16),
             pltpu.VMEM((2, kv_count, window, HEAD_SIZE), bf16),
             pltpu.VMEM((reach + 1, 1, rows), jnp.int32),
             pltpu.VMEM((window, HALF), f32),
-            pltpu.VMEM((rows // HALF, width, HALF), f32),
+            pltpu.VMEM((halves, width, HALF), f32),
             pltpu.VMEM((kv_count, HEAD_SIZE, window), bf16),
             pltpu.VMEM((kv_count, 2, window, HEAD_SIZE), f32),
             pltpu.VMEM((kv_count, reach, 2, rows, HEAD_SIZE), bf16),
             pltpu.VMEM((kv_count, reach, 2, rows, HEAD_SIZE), bf16),
             pltpu.VMEM((kv_count, 2, rows, HEAD_SIZE), bf16),
-            pltpu.VMEM((kv_count, 2, rows, HEAD_SIZE), bf16),
-            dma((2,)),
+            dma((3,)),
             dma((2, kv_count)),
             dma((reach + 1,)),
             dma((reach + 1,)),
@@ -363,13 +423,23 @@
             dma((kv_count, reach)),
             dma((kv_count,)),
             dma((kv_count,)),
-            dma((kv_count,)),
-            dma((2, 2, kv_count)),
         ],
         compiler_params=pltpu.CompilerParams(
-            collective_id=0, has_side_effects=True, vmem_limit_bytes=60 * 1024 * 1024
+            collective_id=0, has_side_effects=True, vmem_limit_bytes=56 * 1024 * 1024
         ),
     )(queries, key_matrix, value_matrix, out_grad, segments.reshape(1, rows))
+    return pl.pallas_call(
+        functools.partial(place, kv_count, shared),
+        out_shape=(
+            jax.ShapeDtypeStruct(queries.shape, bf16),
+            jax.ShapeDtypeStruct(key_matrix.shape, bf16),
+            jax.ShapeDtypeStruct(value_matrix.shape, bf16),
+        ),
+        in_specs=[pl.BlockSpec(memory_space=pltpu.VMEM)] * 3,
+        out_specs=(anywhere,) * 3,
+        scratch_shapes=[dma((1 + 4 * kv_count,))],
+        compiler_params=pltpu.CompilerParams(vmem_limit_bytes=4 * 1024 * 1024),
+    )(dqv, fin, other)
 
 
 def solution(mesh):

time: 46.8 us -> 38.3 us (0.82)
  Pallas kernels: 41.9 us -> 37.5 us
  local copies, waits for them, and re-layouts: 4.1 us -> 0 us
    pallas_call x1, Pallas kernels: 41.9 us -> 36.3 us  [shards(): pl.pallas_call(functools.partial(kernel, n, reach, rows, per_kv, kv_count...]
    unnamed x7 -> x0, local copies, waits for them, and re-layouts: 4.1 us -> none
    pallas_call x0 -> x1, Pallas kernels: none -> 1.2 us  [shards(): pl.pallas_call(functools.partial(place, kv_count, shared), out_shape=(jax...]
where the time goes in v2:
time: 38.3 us; the launch traced here: 38.1 us
  Pallas kernels  37.5 us (98%)
  between operations  0.64 us (2%)
    pallas_call x1, Pallas kernels, shards(): pl.pallas_call(functools.partial(kernel, n, reach, rows, per_kv, kv_count...  36.3 us
    pallas_call x1, Pallas kernels, shards(): pl.pallas_call(functools.partial(place, kv_count, shared), out_shape=(jax...  1.2 us

profile of v2, /device:TPU:0, one launch (start us, length us, event | category | flops | bytes accessed | tf_op | source)
XLA Modules:
  0.0 38.1 jit_solution(1522072190954493832)
XLA Ops:
  0.6 36.3 %shard_map.76 = (bf16[256,2048]{1,0:T(8,128)(2,1)S(1)}, bf16[2,2,256,128]{3,2,1,0:T(8,128)(2,1)S(1)}, bf16[2,2,256,128]{3,2,1,0:T(8,128)(2,1)S(1)}) custom-call(bf16[256,2048]{1,0:T(8,128)(2,1)} %q_hbm.1, bf16[256,512]{1,0:T(8,128)(2,1)} %k_hbm.1, bf16[256,512]{1,0:T(8,128)(2,1)} %v_hbm.1, bf16[256,2048]{1,0:T(8,128)(2,1)} %g_hbm.1, s32[1,256]{1,0:T(1,128)} %bitcast.1), custom_call_target="tpu_custom_call" | custom-call | tf_op jit(solution)/shard_map/pallas_call | solution.py:390
  36.9 1.2 %shard_map.77 = (bf16[256,2048]{1,0:T(8,128)(2,1)}, bf16[256,512]{1,0:T(8,128)(2,1)}, bf16[256,512]{1,0:T(8,128)(2,1)}) custom-call(bf16[256,2048]{1,0:T(8,128)(2,1)S(1)} %get-tuple-element.6.dqv, bf16[2,2,256,128]{3,2,1,0:T(8,128)(2,1)S(1)} %get-tuple-element.7.fin, bf16[2,2,256,128]{3,2,1,0:T(8,128)(2,1)S(1)} %get-tuple-element.8.other), custom_call_target="tpu_custom_call" | custom-call | tf_op jit(solution)/shard_map/pallas_call | solution.py:431

commit v3 on v2

--- a/solution.py
+++ b/solution.py
@@ -79,22 +79,22 @@
             device_id_type=MESH,
         )
 
-    def back(g, d):
+    def back(g, d, t):
         return pltpu.make_async_remote_copy(
-            src_ref=sendb.at[g, d - 1],
-            dst_ref=ret.at[g, d - 1],
-            send_sem=back_send.at[g, d - 1],
-            recv_sem=back_recv.at[g, d - 1],
+            src_ref=sendb.at[g, d - 1, t],
+            dst_ref=ret.at[g, d - 1, t],
+            send_sem=back_send.at[g, d - 1, t],
+            recv_sem=back_recv.at[g, d - 1, t],
             device_id={"ctx": down},
             device_id_type=MESH,
         )
 
-    def to_mate(g):
+    def to_mate(g, t):
         return pltpu.make_async_remote_copy(
-            src_ref=fin.at[g],
-            dst_ref=pfin.at[g],
-            send_sem=pair_send.at[g],
-            recv_sem=pair_recv.at[g],
+            src_ref=fin.at[g, t],
+            dst_ref=pfin.at[g, t],
+            send_sem=pair_send.at[g, t],
+            recv_sem=pair_recv.at[g, t],
             device_id={"kv": mate},
             device_id_type=MESH,
         )
@@ -266,38 +266,35 @@
     def end_units(g):
         grads(g, last_half, pairs - 1)
 
-    def send_back(g, d):
-        if d < reach:
+    def send_first(g):
+        for d in range(reach, 0, -1):
+            @pl.when((rank >= d) if d == reach else jnp.logical_not(has_up))
+            def _(d=d):
+                for t in range(2):
+                    sendb[g, d - 1, t] = acc[g, t, slot(d), :].astype(jnp.bfloat16)
+                    back(g, d, t).start()
+
+    def send_rest(g):
+        for d in range(reach - 1, 0, -1):
             @pl.when(has_up & (rank >= d))
-            def _():
-                back(g, d + 1).wait_recv()
-                sendb[g, d - 1] = (
-                    acc[g, :, slot(d), :] + ret[g, d].astype(jnp.float32)
-                ).astype(jnp.bfloat16)
-
-            @pl.when(jnp.logical_not(has_up) & (rank >= d))
-            def _():
-                sendb[g, d - 1] = acc[g, :, slot(d), :].astype(jnp.bfloat16)
-        else:
-            @pl.when(rank >= d)
-            def _():
-                sendb[g, d - 1] = acc[g, :, slot(d), :].astype(jnp.bfloat16)
-
-        @pl.when(rank >= d)
-        def _():
-            back(g, d).start()
+            def _(d=d):
+                for t in range(2):
+                    back(g, d + 1, t).wait_recv()
+                    sendb[g, d - 1, t] = (
+                        acc[g, t, slot(d), :] + ret[g, d, t].astype(jnp.float32)
+                    ).astype(jnp.bfloat16)
+                    back(g, d, t).start()
 
     def finish(g):
-        @pl.when(has_up)
-        def _():
-            back(g, 1).wait_recv()
-            for t in range(2):
+        for t in range(2):
+            @pl.when(has_up)
+            def _(t=t):
+                back(g, 1, t).wait_recv()
                 acc[g, t, slot(0), :] += ret[g, 0, t].astype(jnp.float32)
 
-        for t in range(2):
             factor = scale if t == 0 else 1.0
             fin[g, t] = (acc[g, t, slot(0), :] * factor).astype(jnp.bfloat16)
-        to_mate(g).start()
+            to_mate(g, t).start()
 
     pass_on_seg()
     seg_load.wait()
@@ -305,30 +302,32 @@
     pass_on(0)
     for copy in loads + owns:
         copy.wait()
-    split = per_kv // 4
+    middle, late = pairs // 2, pairs * 3 // 4
     for g in range(kv_count):
         if g + 1 < kv_count:
             send_own(g + 1)
         last_slot(g)
         kt[g] = win[0, g].T
         begin_units(g)
-        units(g, 0, split)
         if g + 1 < kv_count:
+            units(g, 0, middle)
             pass_on(g + 1)
-        if g > 0:
-            for d in range(reach - 1, 0, -1):
-                send_back(g - 1, d)
-        units(g, split, pairs)
+            units(g, middle, pairs)
+        elif g > 0:
+            units(g, 0, late)
+            send_rest(g - 1)
+            units(g, late, pairs)
+        else:
+            units(g, 0, pairs)
         end_units(g)
-        send_back(g, reach)
-    for d in range(reach - 1, 0, -1):
-        send_back(kv_count - 1, d)
+        send_first(g)
+    send_rest(kv_count - 1)
     for g in range(kv_count):
         finish(g)
 
     for g in range(kv_count):
-        to_mate(g).wait()
         for t in range(2):
+            to_mate(g, t).wait()
             if shared:
                 other[g, t] = (
                     fin[g, t].astype(jnp.float32) + pfin[g, t].astype(jnp.float32)
@@ -346,7 +345,8 @@
         @pl.when(rank >= d)
         def _(d=d):
             for g in range(kv_count):
-                back(g, d).wait_send()
+                for t in range(2):
+                    back(g, d, t).wait_send()
 
 
 def place(kv_count, shared, dqv, fin, other, dq_hbm, dk_hbm, dv_hbm, sem):
@@ -419,10 +419,10 @@
             dma((reach + 1,)),
             dma((2, kv_count, reach + 1)),
             dma((2, kv_count, reach + 1)),
-            dma((kv_count, reach)),
-            dma((kv_count, reach)),
-            dma((kv_count,)),
-            dma((kv_count,)),
+            dma((kv_count, reach, 2)),
+            dma((kv_count, reach, 2)),
+            dma((kv_count, 2)),
+            dma((kv_count, 2)),
         ],
         compiler_params=pltpu.CompilerParams(
             collective_id=0, has_side_effects=True, vmem_limit_bytes=56 * 1024 * 1024

time: 38.3 us -> 36.8 us (0.961)
  Pallas kernels: 37.5 us -> 36 us
    pallas_call x1, Pallas kernels: 36.3 us -> 34.8 us  [shards(): pl.pallas_call(functools.partial(kernel, n, reach, rows, per_kv, kv_count...]
where the time goes in v3:
time: 36.8 us; the launch traced here: 36.6 us
  Pallas kernels  36 us (98%)
  between operations  0.64 us (2%)
    pallas_call x1, Pallas kernels, shards(): pl.pallas_call(functools.partial(kernel, n, reach, rows, per_kv, kv_count...  34.8 us
    pallas_call x1, Pallas kernels, shards(): pl.pallas_call(functools.partial(place, kv_count, shared), out_shape=(jax...  1.2 us

profile of v3, /device:TPU:0, one launch (start us, length us, event | category | flops | bytes accessed | tf_op | source)
XLA Modules:
  0.0 36.6 jit_solution(10393578658100565600)
XLA Ops:
  0.6 34.8 %shard_map.76 = (bf16[256,2048]{1,0:T(8,128)(2,1)S(1)}, bf16[2,2,256,128]{3,2,1,0:T(8,128)(2,1)S(1)}, bf16[2,2,256,128]{3,2,1,0:T(8,128)(2,1)S(1)}) custom-call(bf16[256,2048]{1,0:T(8,128)(2,1)} %q_hbm.1, bf16[256,512]{1,0:T(8,128)(2,1)} %k_hbm.1, bf16[256,512]{1,0:T(8,128)(2,1)} %v_hbm.1, bf16[256,2048]{1,0:T(8,128)(2,1)} %g_hbm.1, s32[1,256]{1,0:T(1,128)} %bitcast.1), custom_call_target="tpu_custom_call" | custom-call | tf_op jit(solution)/shard_map/pallas_call | solution.py:390
  35.4 1.2 %shard_map.77 = (bf16[256,2048]{1,0:T(8,128)(2,1)}, bf16[256,512]{1,0:T(8,128)(2,1)}, bf16[256,512]{1,0:T(8,128)(2,1)}) custom-call(bf16[256,2048]{1,0:T(8,128)(2,1)S(1)} %get-tuple-element.6.dqv, bf16[2,2,256,128]{3,2,1,0:T(8,128)(2,1)S(1)} %get-tuple-element.7.fin, bf16[2,2,256,128]{3,2,1,0:T(8,128)(2,1)S(1)} %get-tuple-element.8.other), custom_call_target="tpu_custom_call" | custom-call | tf_op jit(solution)/shard_map/pallas_call | solution.py:431

commit v4 on v3

--- a/solution.py
+++ b/solution.py
@@ -79,22 +79,30 @@
             device_id_type=MESH,
         )
 
-    def back(g, d, t):
+    pieces = [(t, r) for t in range(2) for r in range(halves)]
+
+    def some(r):
+        return pl.ds(r * HALF, HALF)
+
+    def back(g, d, t, r):
         return pltpu.make_async_remote_copy(
-            src_ref=sendb.at[g, d - 1, t],
-            dst_ref=ret.at[g, d - 1, t],
-            send_sem=back_send.at[g, d - 1, t],
-            recv_sem=back_recv.at[g, d - 1, t],
+            src_ref=sendb.at[g, d - 1, t, some(r)],
+            dst_ref=ret.at[g, d - 1, t, some(r)],
+            send_sem=back_send.at[g, d - 1, t, r],
+            recv_sem=back_recv.at[g, d - 1, t, r],
             device_id={"ctx": down},
             device_id_type=MESH,
         )
 
-    def to_mate(g, t):
+    def owed(g, d, t, r):
+        return acc[g, t, pl.ds((reach - d) * rows + r * HALF, HALF), :]
+
+    def to_mate(g, t, r):
         return pltpu.make_async_remote_copy(
-            src_ref=fin.at[g, t],
-            dst_ref=pfin.at[g, t],
-            send_sem=pair_send.at[g, t],
-            recv_sem=pair_recv.at[g, t],
+            src_ref=fin.at[g, t, some(r)],
+            dst_ref=pfin.at[g, t, some(r)],
+            send_sem=pair_send.at[g, t, r],
+            recv_sem=pair_recv.at[g, t, r],
             device_id={"kv": mate},
             device_id_type=MESH,
         )
@@ -145,9 +153,9 @@
                 def _(d=d):
                     forward_seg(d).start()
 
-    def pass_on(g):
+    def pass_on(g, kinds):
         for d in range(1, reach):
-            for t in range(2):
+            for t in kinds:
                 @pl.when(rank >= d)
                 def _(d=d, t=t):
                     forward(t, g, d - 1).wait_recv()
@@ -270,39 +278,41 @@
         for d in range(reach, 0, -1):
             @pl.when((rank >= d) if d == reach else jnp.logical_not(has_up))
             def _(d=d):
-                for t in range(2):
-                    sendb[g, d - 1, t] = acc[g, t, slot(d), :].astype(jnp.bfloat16)
-                    back(g, d, t).start()
+                for t, r in pieces:
+                    sendb[g, d - 1, t, some(r), :] = owed(g, d, t, r).astype(jnp.bfloat16)
+                    back(g, d, t, r).start()
 
     def send_rest(g):
         for d in range(reach - 1, 0, -1):
             @pl.when(has_up & (rank >= d))
             def _(d=d):
-                for t in range(2):
-                    back(g, d + 1, t).wait_recv()
-                    sendb[g, d - 1, t] = (
-                        acc[g, t, slot(d), :] + ret[g, d, t].astype(jnp.float32)
+                for t, r in pieces:
+                    back(g, d + 1, t, r).wait_recv()
+                    sendb[g, d - 1, t, some(r), :] = (
+                        owed(g, d, t, r) + ret[g, d, t, some(r), :].astype(jnp.float32)
                     ).astype(jnp.bfloat16)
-                    back(g, d, t).start()
+                    back(g, d, t, r).start()
 
     def finish(g):
-        for t in range(2):
+        for t, r in pieces:
             @pl.when(has_up)
-            def _(t=t):
-                back(g, 1, t).wait_recv()
-                acc[g, t, slot(0), :] += ret[g, 0, t].astype(jnp.float32)
+            def _(t=t, r=r):
+                back(g, 1, t, r).wait_recv()
+                acc[g, t, pl.ds(reach * rows + r * HALF, HALF), :] += (
+                    ret[g, 0, t, some(r), :].astype(jnp.float32)
+                )
 
             factor = scale if t == 0 else 1.0
-            fin[g, t] = (acc[g, t, slot(0), :] * factor).astype(jnp.bfloat16)
-            to_mate(g, t).start()
+            fin[g, t, some(r), :] = (owed(g, 0, t, r) * factor).astype(jnp.bfloat16)
+            to_mate(g, t, r).start()
 
     pass_on_seg()
     seg_load.wait()
     make_bias()
-    pass_on(0)
+    pass_on(0, (0, 1))
     for copy in loads + owns:
         copy.wait()
-    middle, late = pairs // 2, pairs * 3 // 4
+    early, middle, late = pairs // 4, pairs // 2, pairs * 3 // 4
     for g in range(kv_count):
         if g + 1 < kv_count:
             send_own(g + 1)
@@ -310,8 +320,12 @@
         kt[g] = win[0, g].T
         begin_units(g)
         if g + 1 < kv_count:
-            units(g, 0, middle)
-            pass_on(g + 1)
+            units(g, 0, early)
+            pass_on(g + 1, (0,))
+            units(g, early, middle)
+            pass_on(g + 1, (1,))
+            if g > 0:
+                send_rest(g - 1)
             units(g, middle, pairs)
         elif g > 0:
             units(g, 0, late)
@@ -327,7 +341,8 @@
 
     for g in range(kv_count):
         for t in range(2):
-            to_mate(g, t).wait()
+            for r in range(halves):
+                to_mate(g, t, r).wait()
             if shared:
                 other[g, t] = (
                     fin[g, t].astype(jnp.float32) + pfin[g, t].astype(jnp.float32)
@@ -345,8 +360,8 @@
         @pl.when(rank >= d)
         def _(d=d):
             for g in range(kv_count):
-                for t in range(2):
-                    back(g, d, t).wait_send()
+                for t, r in pieces:
+                    back(g, d, t, r).wait_send()
 
 
 def place(kv_count, shared, dqv, fin, other, dq_hbm, dk_hbm, dv_hbm, sem):
@@ -419,10 +434,10 @@
             dma((reach + 1,)),
             dma((2, kv_count, reach + 1)),
             dma((2, kv_count, reach + 1)),
-            dma((kv_count, reach, 2)),
-            dma((kv_count, reach, 2)),
-            dma((kv_count, 2)),
-            dma((kv_count, 2)),
+            dma((kv_count, reach, 2, halves)),
+            dma((kv_count, reach, 2, halves)),
+            dma((kv_count, 2, halves)),
+            dma((kv_count, 2, halves)),
         ],
         compiler_params=pltpu.CompilerParams(
             collective_id=0, has_side_effects=True, vmem_limit_bytes=56 * 1024 * 1024

time: 36.8 us -> 36.4 us (0.989)
  Pallas kernels: 36 us -> 35.6 us
where the time goes in v4:
time: 36.4 us; the launch traced here: 36.3 us
  Pallas kernels  35.6 us (98%)
  between operations  0.64 us (2%)
    pallas_call x1, Pallas kernels, shards(): pl.pallas_call(functools.partial(kernel, n, reach, rows, per_kv, kv_count...  34.4 us
    pallas_call x1, Pallas kernels, shards(): pl.pallas_call(functools.partial(place, kv_count, shared), out_shape=(jax...  1.2 us

profile of v4, /device:TPU:0, one launch (start us, length us, event | category | flops | bytes accessed | tf_op | source)
XLA Modules:
  0.0 36.3 jit_solution(13721364882528985506)
XLA Ops:
  0.6 34.4 %shard_map.76 = (bf16[256,2048]{1,0:T(8,128)(2,1)S(1)}, bf16[2,2,256,128]{3,2,1,0:T(8,128)(2,1)S(1)}, bf16[2,2,256,128]{3,2,1,0:T(8,128)(2,1)S(1)}) custom-call(bf16[256,2048]{1,0:T(8,128)(2,1)} %q_hbm.1, bf16[256,512]{1,0:T(8,128)(2,1)} %k_hbm.1, bf16[256,512]{1,0:T(8,128)(2,1)} %v_hbm.1, bf16[256,2048]{1,0:T(8,128)(2,1)} %g_hbm.1, s32[1,256]{1,0:T(1,128)} %bitcast.1), custom_call_target="tpu_custom_call" | custom-call | tf_op jit(solution)/shard_map/pallas_call | solution.py:405
  35.1 1.2 %shard_map.77 = (bf16[256,2048]{1,0:T(8,128)(2,1)}, bf16[256,512]{1,0:T(8,128)(2,1)}, bf16[256,512]{1,0:T(8,128)(2,1)}) custom-call(bf16[256,2048]{1,0:T(8,128)(2,1)S(1)} %get-tuple-element.6.dqv, bf16[2,2,256,128]{3,2,1,0:T(8,128)(2,1)S(1)} %get-tuple-element.7.fin, bf16[2,2,256,128]{3,2,1,0:T(8,128)(2,1)S(1)} %get-tuple-element.8.other), custom_call_target="tpu_custom_call" | custom-call | tf_op jit(solution)/shard_map/pallas_call | solution.py:446
